TPU v7x, 32 devices: a whole 2x2x4 slice. The times are simulated.
32 devices in a mesh: img: 4 (over y, core), pix: 8 (over z, x).
Axes of the slice: x: 2, y: 2, z: 4, core: 2. Of those that a mesh axis runs over, the one named last changes fastest.
Arguments:
- pixels: float32 [2, 4, 82944, 261], P(None, 'img', 'pix'), may hold values from -6 to 6
- sides: int32 [2], replicated, may hold values from 160 to 288, as said below
- owner: int32 [256], replicated, may hold values from 0 to 255, each once
- master: float32 [256, 128, 128], P(('img', 'pix')), may hold values from -0.375 to 0.375
- left_stat: float32 [256, 128, 128], P(('img', 'pix'))
- right_stat: float32 [256, 128, 128], P(('img', 'pix'))
- left_root: float32 [256, 128, 128], P(('img', 'pix'))
- right_root: float32 [256, 128, 128], P(('img', 'pix'))
- kv_weight: float32 [2, 261, 1024], replicated, may hold values from -0.375 to 0.375
- latent_array: float32 [512, 1024], replicated, may hold values from -6 to 6
- in_gain: float32 [261], replicated, may hold values from 0.5 to 1.5
- lat_gains: float32 [2, 1024], replicated, may hold values from 0.5 to 1.5
- cotangent: float32 [2, 4, 512, 1024], P(None, 'img', 'pix'), may hold values from -6 to 6
Outputs:
- latents_out: float32 [2, 4, 512, 1024], P(None, 'img', 'pix')
- pixel_grad: float32 [2, 4, 82944, 261], P(None, 'img', 'pix')
- new_left: float32 [256, 128, 128], P(('img', 'pix'))
- new_right: float32 [256, 128, 128], P(('img', 'pix'))
- new_master: float32 [256, 128, 128], P(('img', 'pix'))
- new_copy: bfloat16 [256, 128, 128], P(('img', 'pix'))
- kv_grad: float32 [2, 261, 1024], replicated
- new_kv: float32 [2, 261, 1024], replicated
- latent_grad: float32 [512, 1024], replicated
- new_latent: float32 [512, 1024], replicated
- in_gain_grad: float32 [261], replicated
- new_in_gain: float32 [261], replicated
- lat_gain_grad: float32 [2, 1024], replicated
- new_lat_gains: float32 [2, 1024], replicated
Inputs may be any that keep to these rules, and one draw needn't show every extreme that they name: Every image of micro-batch m is sides[m] pixels a side, one of 160, 224 or 288; some micro-batch has 288 and some has a smaller side. Slot p of an image (row by row) is a real pixel when p < sides[m]^2; the rest of the 82944 slots are padding. A permutation: block b lives in slot owner[b]; the slots run in order over the devices of img+pix, an equal number to each.
All inputs are finite; a program needn't handle non-finite values.
Results may differ from a plain program's by a relative error of at most 0.015.
The roundings to bfloat16 on the way count: a program that leaves them out, or rounds other values in their place, can miss the bound.
Values may be sent and summed in bfloat16 or wider, within the bound.
No kernel may reach another device: no remote copies, remote signals or barrier semaphores. Data moves between devices by JAX's collectives and lax.ppermute only.
A program may use at most 448 MiB of HBM per device.

v0:
```python
import math

import jax
import jax.numpy as jnp
from jax import lax
from jax.experimental import pallas as pl
from jax.experimental.pallas import tpu as pltpu
from jax.sharding import PartitionSpec as P

CIN = 261
DL = 1024
LAT = 512
BLK = 128
NBLK = 256
PER_MATRIX = NBLK // 4
CEXT = 264
ONES_ROW = 261
MASK_ROW = 263
MASKED = -1e30

HIGHEST_PRECISION = lax.Precision.HIGHEST


def standardize(values_in):
    average = jnp.mean(values_in, axis=-1, keepdims=True)
    centred = values_in - average
    variance = jnp.mean(centred * centred, axis=-1, keepdims=True)
    return centred * lax.rsqrt(variance + 1e-05)


def gelu_exact(values_in):
    return jax.nn.gelu(values_in, approximate=False)


def normalized(gradient, reduce_axes):
    return gradient / jnp.sqrt(
        jnp.mean(gradient * gradient, axis=reduce_axes, keepdims=True) + 1e-06
    )


def product(pattern, left_side, right_side):
    return jnp.einsum(pattern, left_side, right_side, preferred_element_type=jnp.float32)


def fine(pattern, left_side, right_side):
    return jnp.einsum(
        pattern,
        left_side.astype(jnp.float32),
        right_side.astype(jnp.float32),
        precision=HIGHEST_PRECISION,
    )


def two_terms(values_in):
    head = lax.reduce_precision(values_in, 8, 7)
    return (head.astype(jnp.bfloat16), (values_in - head).astype(jnp.bfloat16))


def contract_rows(left_side, right_side, precision=None):
    return lax.dot_general(
        left_side,
        right_side,
        (((0,), (0,)), ((), ())),
        precision=precision,
        preferred_element_type=jnp.float32,
    )


def dot(left_side, right_side):
    return jnp.dot(left_side, right_side, preferred_element_type=jnp.float32)


def dot_last(left_side, right_side):
    return lax.dot_general(
        left_side, right_side, (((1,), (1,)), ((), ())), preferred_element_type=jnp.float32
    )


def tile_of(rows, most):
    return max((size for size in range(128, most + 1, 128) if rows % size == 0), default=rows)


def lies_across(pixels):
    micro, _, rows_dev, _ = pixels.shape
    return jnp.swapaxes(pixels, 2, 3).reshape(micro, CIN, 1, rows_dev)


def centre(pix):
    centred = pix - jnp.mean(pix, axis=0, keepdims=True)
    scale = lax.rsqrt(jnp.mean(centred * centred, axis=0, keepdims=True) + 1e-05)
    return (centred * scale, scale)


def cost(flops, count):
    return pl.CostEstimate(flops=int(flops), bytes_accessed=int(count), transcendentals=0)


def prepare_body(place_ref, pix_ref, gain_ref, out_ref):
    micro_index = pl.program_id(0)
    normed, _ = centre(pix_ref[0, :, 0, :])
    columns = normed.shape[1]
    extra = (CEXT - CIN, columns)
    slot = place_ref[0] + pl.program_id(1) * columns + lax.broadcasted_iota(jnp.int32, extra, 1)
    row = lax.broadcasted_iota(jnp.int32, extra, 0) + CIN
    mask = jnp.where(slot < place_ref[1 + micro_index], 0.0, MASKED)
    tail = jnp.where(row == MASK_ROW, mask, 1.0)
    out_ref[0] = jnp.concatenate([normed * gain_ref[...], tail], axis=0).astype(jnp.bfloat16)


def prepare_pixels(place, across, gain_column):
    micro, _, _, rows_dev = across.shape
    rows = tile_of(rows_dev, 1152)
    return pl.pallas_call(
        prepare_body,
        grid=(micro, rows_dev // rows),
        in_specs=[
            pl.BlockSpec(memory_space=pltpu.SMEM),
            pl.BlockSpec((1, CIN, 1, rows), lambda m, t: (m, 0, 0, t)),
            pl.BlockSpec((CIN, 1), lambda m, t: (0, 0)),
        ],
        out_specs=pl.BlockSpec((1, CEXT, rows), lambda m, t: (m, 0, t)),
        out_shape=jax.ShapeDtypeStruct((micro, CEXT, rows_dev), jnp.bfloat16),
        cost_estimate=cost(0, 6 * micro * rows_dev * CEXT),
        name="prepare_pixels",
    )(place, across, gain_column)


def attend_body(feat_ref, query_ref, exp_ref, out_ref, sum_ref):
    tile = pl.program_id(1)
    feats = feat_ref[0]
    weights = jnp.exp(contract_rows(feats, query_ref[...])).astype(jnp.bfloat16)
    exp_ref[0] = weights

    @pl.when(tile == 0)
    def _():
        sum_ref[...] = jnp.zeros_like(sum_ref)

    sum_ref[...] += dot(feats, weights)

    @pl.when(tile == pl.num_programs(1) - 1)
    def _():
        sums = sum_ref[...]
        low = sums.astype(jnp.bfloat16)
        rest = (sums - low.astype(jnp.float32))[ONES_ROW : ONES_ROW + 1]
        row = lax.broadcasted_iota(jnp.int32, sums.shape, 0)
        out_ref[0] = jnp.where(row == ONES_ROW + 1, rest, sums).astype(jnp.bfloat16)


def attend(feats, query_cols):
    micro, _, rows_dev = feats.shape
    rows = tile_of(rows_dev, 1152)
    return pl.pallas_call(
        attend_body,
        grid=(micro, rows_dev // rows),
        in_specs=[
            pl.BlockSpec((1, CEXT, rows), lambda m, t: (m, 0, t)),
            pl.BlockSpec((CEXT, LAT), lambda m, t: (0, 0)),
        ],
        out_specs=[
            pl.BlockSpec((1, rows, LAT), lambda m, t: (m, t, 0)),
            pl.BlockSpec((1, CEXT, LAT), lambda m, t: (m, 0, 0)),
        ],
        out_shape=[
            jax.ShapeDtypeStruct((micro, rows_dev, LAT), jnp.bfloat16),
            jax.ShapeDtypeStruct((micro, CEXT, LAT), jnp.bfloat16),
        ],
        scratch_shapes=[pltpu.VMEM((CEXT, LAT), jnp.float32)],
        cost_estimate=cost(8 * micro * rows_dev * LAT * CEXT, 4 * micro * rows_dev * LAT),
        name="attend",
    )(feats, query_cols)


def attend_back_body(pix_ref, feat_ref, exp_ref, gain_ref, dc_ref, qc_ref, *rest):
    grad_ref, score_ref, gain_sum_ref = rest[-3:]
    feats = feat_ref[0]
    weights = exp_ref[0]
    d_exp = contract_rows(feats, dc_ref[0])
    d_scores = (weights.astype(jnp.float32) * d_exp).astype(jnp.bfloat16)

    @pl.when(pl.program_id(0) == 0)
    def _():
        score_ref[...] = jnp.zeros_like(score_ref)
        gain_sum_ref[...] = jnp.zeros_like(gain_sum_ref)

    score_ref[...] += dot(feats, d_scores)
    d_pix = (dot_last(qc_ref[...], d_scores) + dot_last(dc_ref[0], weights))[:CIN]
    normed, scale = centre(pix_ref[0, :, 0, :])
    gain_sum_ref[...] += jnp.sum(d_pix * normed, axis=1, keepdims=True)
    d_normed = d_pix * gain_ref[...]
    along = jnp.mean(d_normed * normed, axis=0, keepdims=True)
    level = jnp.mean(d_normed, axis=0, keepdims=True)
    grad_ref[0, :, 0, :] = (d_normed - level - normed * along) * scale


def attend_back(micro_index, earlier, across, feats, weights, gain_column, d_cols, query_cols):
    rows_dev = feats.shape[2]
    rows = tile_of(rows_dev, 1152)
    m = micro_index
    in_specs = [
        pl.BlockSpec((1, CIN, 1, rows), lambda t: (m, 0, 0, t)),
        pl.BlockSpec((1, CEXT, rows), lambda t: (m, 0, t)),
        pl.BlockSpec((1, rows, LAT), lambda t: (m, t, 0)),
        pl.BlockSpec((CIN, 1), lambda t: (0, 0)),
        pl.BlockSpec((1, CEXT, LAT), lambda t: (m, 0, 0)),
        pl.BlockSpec((CEXT, LAT), lambda t: (0, 0)),
    ]
    operands = [across, feats, weights, gain_column, d_cols, query_cols]
    aliases = {}
    if earlier is not None:
        in_specs.append(pl.BlockSpec(memory_space=pl.ANY))
        aliases = {len(operands): 0}
        operands.append(earlier)
    return pl.pallas_call(
        attend_back_body,
        grid=(rows_dev // rows,),
        in_specs=in_specs,
        out_specs=[
            pl.BlockSpec((1, CIN, 1, rows), lambda t: (m, 0, 0, t)),
            pl.BlockSpec((CEXT, LAT), lambda t: (0, 0)),
            pl.BlockSpec((CIN, 1), lambda t: (0, 0)),
        ],
        out_shape=[
            jax.ShapeDtypeStruct(across.shape, jnp.float32),
            jax.ShapeDtypeStruct((CEXT, LAT), jnp.float32),
            jax.ShapeDtypeStruct((CIN, 1), jnp.float32),
        ],
        input_output_aliases=aliases,
        cost_estimate=cost(16 * rows_dev * LAT * CEXT, rows_dev * 4000),
        name="attend_back",
    )(*operands)


def query_body(owner_ref, blocks_ref, lat_ref, gain_ref, key_ref, *rest):
    low_ref, query_ref, cols_ref, wq_ref, wo_ref, w1_ref, w2_ref, square_ref, sems = rest
    side = DL // BLK

    def fetch(matrix, target_ref):
        @pl.loop(0, PER_MATRIX)
        def _(block):
            row = pl.multiple_of((block // side) * BLK, BLK)
            column = pl.multiple_of((block % side) * BLK, BLK)
            pltpu.make_async_copy(
                blocks_ref.at[owner_ref[matrix * PER_MATRIX + block]],
                target_ref.at[pl.ds(row, BLK), pl.ds(column, BLK)],
                sems.at[matrix],
            ).start()

    def settle(matrix, target_ref):
        pltpu.make_async_copy(target_ref, target_ref, sems.at[matrix]).wait()

    fetch(0, square_ref)
    for matrix, target_ref in ((1, wo_ref), (2, w1_ref), (3, w2_ref)):
        fetch(matrix, target_ref)
    lat_low = (standardize(lat_ref[...]) * gain_ref[...]).astype(jnp.bfloat16)
    low_ref[...] = lat_low
    settle(0, square_ref)
    keep = pltpu.make_async_copy(square_ref, wq_ref, sems.at[0])
    keep.start()
    query = dot(lat_low, square_ref[...]).astype(jnp.bfloat16)
    query_ref[...] = query
    scores = dot_last(key_ref[...], query) * (1.0 / math.sqrt(DL))
    row = lax.broadcasted_iota(jnp.int32, (CEXT - CIN, LAT), 0) + CIN
    tail = jnp.where(row == MASK_ROW, 1.0, 0.0)
    cols_ref[...] = jnp.concatenate([scores, tail], axis=0).astype(jnp.bfloat16)
    keep.wait()
    for matrix, target_ref in ((1, wo_ref), (2, w1_ref), (3, w2_ref)):
        settle(matrix, target_ref)


def make_query(owner, gathered, latent_array, gain, w_key):
    vmem = pl.BlockSpec(memory_space=pltpu.VMEM)
    hbm = pl.BlockSpec(memory_space=pl.ANY)
    rows = jax.ShapeDtypeStruct((LAT, DL), jnp.bfloat16)
    square = jax.ShapeDtypeStruct((DL, DL), jnp.bfloat16)
    return pl.pallas_call(
        query_body,
        in_specs=[pl.BlockSpec(memory_space=pltpu.SMEM), hbm, vmem, vmem, vmem],
        out_specs=[vmem] * 3 + [hbm] * 4,
        out_shape=[rows, rows, jax.ShapeDtypeStruct((CEXT, LAT), jnp.bfloat16)] + [square] * 4,
        scratch_shapes=[pltpu.VMEM((DL, DL), jnp.bfloat16), pltpu.SemaphoreType.DMA((4,))],
        cost_estimate=cost(3 * LAT * DL * DL, 4 * NBLK * BLK * BLK),
        name="make_query",
    )(owner, gathered, latent_array, gain[None], w_key)


def slot_grads_body(where_ref, left_ref, right_ref, keep_ref, send_ref, full_ref, zero_ref, sems):
    half = NBLK // 2
    side = DL // BLK

    def put(source, block):
        place = where_ref[block]

        @pl.when(place < half)
        def _():
            pltpu.make_async_copy(source, keep_ref.at[place], sems.at[0]).start()

        @pl.when(place >= half)
        def _():
            pltpu.make_async_copy(source, send_ref.at[place - half], sems.at[1]).start()

    zero_ref[...] = jnp.zeros_like(zero_ref)

    @pl.loop(0, PER_MATRIX)
    def _(block):
        put(zero_ref, block)

    for matrix in range(3):
        full_ref[matrix] = contract_rows(left_ref[matrix], right_ref[matrix]).astype(jnp.bfloat16)

        @pl.loop(0, PER_MATRIX)
        def _(block, matrix=matrix):
            row = pl.multiple_of((block // side) * BLK, BLK)
            column = pl.multiple_of((block % side) * BLK, BLK)
            put(
                full_ref.at[matrix, pl.ds(row, BLK), pl.ds(column, BLK)],
                (matrix + 1) * PER_MATRIX + block,
            )

    pltpu.make_async_copy(keep_ref, keep_ref, sems.at[0]).wait()
    pltpu.make_async_copy(send_ref, send_ref, sems.at[1]).wait()


def slot_grads(where, left_rows, right_rows):
    half = jax.ShapeDtypeStruct((NBLK // 2, BLK, BLK), jnp.bfloat16)
    return pl.pallas_call(
        slot_grads_body,
        in_specs=[
            pl.BlockSpec(memory_space=pltpu.SMEM),
            pl.BlockSpec(memory_space=pltpu.VMEM),
            pl.BlockSpec(memory_space=pltpu.VMEM),
        ],
        out_specs=[pl.BlockSpec(memory_space=pl.ANY)] * 2,
        out_shape=[half, half],
        scratch_shapes=[
            pltpu.VMEM((3, DL, DL), jnp.bfloat16),
            pltpu.VMEM((BLK, BLK), jnp.bfloat16),
            pltpu.SemaphoreType.DMA((2,)),
        ],
        name="slot_grads",
    )(where, left_rows, right_rows)


def update_body(block_ref, lat_ref, dq_ref, sum_ref, ls_ref, rs_ref, lr_ref, rr_ref, ma_ref, *outs):
    new_left, new_right, new_master, new_copy = outs

    def exact(left_side, right_side, dims):
        return lax.dot_general(
            left_side,
            right_side,
            (dims, ((), ())),
            precision=HIGHEST_PRECISION,
            preferred_element_type=jnp.float32,
        )

    is_query = block_ref[pl.program_id(0)] < PER_MATRIX
    grad = jnp.where(is_query, contract_rows(lat_ref[...], dq_ref[...]), sum_ref[0])
    new_left[0] = 0.5 * ls_ref[0] + 0.5 * exact(grad, grad, ((1,), (1,)))
    new_right[0] = 0.5 * rs_ref[0] + 0.5 * exact(grad, grad, ((0,), (0,)))
    half_step = exact(lr_ref[0], grad, ((1,), (0,)))
    shampoo = exact(half_step, rr_ref[0], ((1,), (0,)))
    mean_square = jnp.mean(shampoo * shampoo)
    updated = ma_ref[0] - 0.5 / math.sqrt(DL) * (shampoo / jnp.sqrt(mean_square + 1e-06))
    new_master[0] = updated
    new_copy[0] = updated.astype(jnp.bfloat16)


def update_slots(blocks, lat_low, d_query, sums, left_stat, right_stat, left_root, right_root, master):
    slots = master.shape[0]
    side = DL // BLK
    spec = pl.BlockSpec((1, BLK, BLK), lambda s, block: (s, 0, 0))

    def query_block(s, block):
        return jnp.where(block[s] < PER_MATRIX, block[s], 0)

    shape = jax.ShapeDtypeStruct(master.shape, jnp.float32)
    return pl.pallas_call(
        update_body,
        grid_spec=pltpu.PrefetchScalarGridSpec(
            num_scalar_prefetch=1,
            grid=(slots,),
            in_specs=[
                pl.BlockSpec((LAT, BLK), lambda s, block: (0, query_block(s, block) // side)),
                pl.BlockSpec((LAT, BLK), lambda s, block: (0, query_block(s, block) % side)),
            ]
            + [spec] * 6,
            out_specs=[spec] * 4,
        ),
        out_shape=[shape, shape, shape, jax.ShapeDtypeStruct(master.shape, jnp.bfloat16)],
        name="update_slots",
    )(blocks, lat_low, d_query, sums, left_stat, right_stat, left_root, right_root, master)


def swap(array, axis):
    return lax.all_to_all(array, axis, 0, 0, tiled=True)


def everyone(array, axis):
    return swap(jnp.broadcast_to(array[None], (lax.axis_size(axis), *array.shape)), axis)


def total_of(partial):
    rows, width = partial.shape
    n_pix = lax.axis_size("pix")
    each = -(-rows // n_pix)
    padded = jnp.pad(partial.astype(jnp.bfloat16), ((0, each * n_pix - rows), (0, 0)))
    part = jnp.sum(swap(padded.reshape(n_pix, each, width), "pix").astype(jnp.float32), axis=0)
    part = jnp.sum(everyone(part, "img"), axis=0).astype(jnp.bfloat16)
    return everyone(part, "pix").reshape(n_pix * each, width)[:rows]


def add_low(left_side, right_side):
    return (left_side.astype(jnp.float32) + right_side.astype(jnp.float32)).astype(jnp.bfloat16)


def latent_pass(numerator, denominator, lat_part, cot_rows, lat_gain, w_out, w_up, w_down):
    attended = numerator / denominator[..., None]
    att_low = attended.astype(jnp.bfloat16)
    resid = lat_part[None] + product("mrd,de->mre", att_low, w_out)
    normed, normed_back = jax.vjp(standardize, resid)
    hn_low = (normed * lat_gain).astype(jnp.bfloat16)
    hidden = product("mrd,de->mre", hn_low, w_up)
    active, active_back = jax.vjp(gelu_exact, hidden)
    act_low = active.astype(jnp.bfloat16)
    latents_out = resid + product("mrd,de->mre", act_low, w_down)
    g_mlp = cot_rows.astype(jnp.bfloat16)
    d_active = product("mre,de->mrd", g_mlp, w_down)
    d_hidden = active_back(d_active)[0].astype(jnp.bfloat16)
    d_normed = product("mre,de->mrd", d_hidden, w_up)
    d_resid = cot_rows + normed_back(d_normed * lat_gain)[0]
    d_branch = d_resid.astype(jnp.bfloat16)
    d_attended = product("mre,de->mrd", d_branch, w_out)
    d_numer = d_attended / denominator[..., None]
    d_denom = -jnp.sum(d_attended * numerator / (denominator * denominator)[..., None], axis=-1)
    left_rows = jnp.stack([att_low, hn_low, act_low]).reshape(3, -1, DL)
    right_rows = jnp.stack([d_branch, d_hidden, g_mlp]).reshape(3, -1, DL)
    gain_mlp = jnp.sum(d_normed * normed, axis=(0, 1))
    lat_resid = jnp.sum(d_resid, axis=0)
    return (
        latents_out,
        d_numer.astype(jnp.bfloat16),
        d_denom,
        (left_rows, right_rows, gain_mlp, lat_resid),
    )


def shards(
    pixels,
    sides,
    owner,
    master,
    left_stat,
    right_stat,
    left_root,
    right_root,
    kv_weight,
    latent_array,
    in_gain,
    lat_gains,
    cotangent,
):
    micro = pixels.shape[0]
    rows_dev = pixels.shape[2]
    n_pix = lax.axis_size("pix")
    n_img = lax.axis_size("img")
    img = lax.axis_index("img")
    pix = lax.axis_index("pix")
    slots_dev = master.shape[0]
    lat_rows = LAT // n_pix
    row_start = pix * lat_rows
    inv_root = 1.0 / math.sqrt(DL)

    place = jnp.concatenate([(pix * rows_dev)[None], sides * sides]).astype(jnp.int32)
    gathered = lax.all_gather(master.astype(jnp.bfloat16), ("img", "pix"), axis=0, tiled=True)
    across = lies_across(pixels)
    gain_column = in_gain[:, None]
    feats = prepare_pixels(place, across, gain_column)
    kv_low = kv_weight.astype(jnp.bfloat16)
    w_key, w_value = (kv_low[0], kv_low[1])
    lat_norm, lat_norm_back = jax.vjp(standardize, latent_array)
    lat_low, query, query_cols, w_query, w_out, w_up, w_down = make_query(
        owner, gathered, latent_array, lat_gains[0], w_key
    )

    weights, sums = attend(feats, query_cols)
    sums = sums.reshape(micro, CEXT, n_pix, lat_rows).transpose(2, 1, 0, 3)
    sums = swap(sums.reshape(n_pix, CEXT, micro * lat_rows), "pix")
    sums = jnp.sum(sums.astype(jnp.float32), axis=0)
    numer_in = sums[:CIN]
    denominator = (sums[ONES_ROW] + sums[ONES_ROW + 1]).reshape(micro, lat_rows)
    numerator = fine("cr,cd->rd", numer_in, w_value).reshape(micro, lat_rows, DL)
    latents_out, d_numer, d_denom, latent_grads = latent_pass(
        numerator,
        denominator,
        lax.dynamic_slice_in_dim(latent_array, row_start, lat_rows, 0),
        cotangent[:, 0],
        lat_gains[1],
        w_out,
        w_up,
        w_down,
    )
    left_rows, right_rows, gain_mlp, lat_resid = latent_grads
    d_numer = d_numer.reshape(micro * lat_rows, DL)
    head, rest = two_terms(d_denom.reshape(1, micro * lat_rows))
    d_cols = product("rd,cd->cr", d_numer, w_value).astype(jnp.bfloat16)
    d_cols = jnp.concatenate([d_cols, head, rest, jnp.zeros_like(head)], axis=0)
    d_cols = everyone(d_cols, "pix").reshape(n_pix, CEXT, micro, lat_rows)
    d_cols = d_cols.transpose(2, 1, 0, 3).reshape(micro, CEXT, LAT)

    device_of = owner // slots_dev
    img_of = device_of // n_pix
    n_far = n_img // 2
    far_step = (img_of // 2 - img // 2) % n_far
    where = (far_step * n_pix + device_of % n_pix) * slots_dev + owner % slots_dev
    where = where + jnp.where(img_of % 2 == img % 2, 0, NBLK // 2)
    keep, send = slot_grads(where.astype(jnp.int32), left_rows, right_rows)
    got = lax.ppermute(send, "img", [(i, i ^ 1) for i in range(n_img)])
    count = NBLK // 2 // n_far
    pieces = [
        add_low(keep[k * count : (k + 1) * count], got[k * count : (k + 1) * count])
        for k in range(n_far)
    ]
    grads = pieces[0].astype(jnp.float32)
    for k in range(1, n_far):
        hop = [(i, (i + 2 * k) % n_img) for i in range(n_img)]
        grads = grads + lax.ppermute(pieces[k], "img", hop).astype(jnp.float32)

    value_grad = fine("cr,rd->cd", numer_in, d_numer)
    early = jnp.concatenate([value_grad, gain_mlp[None]], axis=0)

    results = (None,)
    score_sum = jnp.zeros((CEXT, LAT), jnp.float32)
    gain_sum = jnp.zeros((CIN, 1), jnp.float32)
    for micro_index in range(micro):
        results = attend_back(
            micro_index, results[0], across, feats, weights, gain_column, d_cols, query_cols
        )
        score_sum = score_sum + results[1]
        gain_sum = gain_sum + results[2]
    pixel_grad = jnp.swapaxes(results[0].reshape(micro, 1, CIN, rows_dev), 2, 3)

    early_total = total_of(early).astype(jnp.float32)
    value_total = early_total[:CIN]
    gain_mlp_total = early_total[CIN]
    lat_part = jnp.sum(everyone(lat_resid.astype(jnp.bfloat16), "img").astype(jnp.float32), axis=0)
    resid_total = everyone(lat_part.astype(jnp.bfloat16), "pix").reshape(LAT, DL)

    late = jnp.concatenate([score_sum[:CIN], jnp.pad(gain_sum.T, ((0, 0), (0, LAT - CIN)))], axis=0)
    late_total = total_of(late)
    score_total = late_total[:CIN]
    in_gain_grad = late_total[CIN, :CIN].astype(jnp.float32)

    grads = grads.astype(jnp.bfloat16).reshape(n_pix * slots_dev, BLK, BLK)
    grads = swap(grads, "pix").reshape(n_pix, slots_dev, BLK, BLK)
    grads = jnp.sum(grads.astype(jnp.float32), axis=0)

    d_query = (contract_rows(score_total, w_key) * inv_root).astype(jnp.bfloat16)
    key_total = dot(score_total, query) * inv_root
    kv_grad = jnp.stack([key_total, value_total])
    d_lat_norm = product("le,de->ld", d_query, w_query)
    latent_grad = resid_total.astype(jnp.float32) + lat_norm_back(d_lat_norm * lat_gains[0])[0]
    lat_gain_grad = jnp.stack([jnp.sum(d_lat_norm * lat_norm, axis=0), gain_mlp_total])

    mine = (img * n_pix + pix) * slots_dev + jnp.arange(slots_dev, dtype=jnp.int32)
    blocks = jnp.sum(
        jnp.where(owner[None] == mine[:, None], jnp.arange(NBLK, dtype=jnp.int32)[None], 0), axis=1
    )
    new_left, new_right, new_master, new_copy = update_slots(
        blocks.astype(jnp.int32),
        lat_low,
        d_query,
        grads,
        left_stat,
        right_stat,
        left_root,
        right_root,
        master,
    )
    new_kv = kv_weight - 0.3 / math.sqrt(CIN) * normalized(kv_grad, (1, 2))
    new_latent = latent_array - 0.3 * normalized(latent_grad, (0, 1))
    new_in_gain = in_gain - 0.2 * normalized(in_gain_grad, (0,))
    new_lat_gains = lat_gains - 0.2 * normalized(lat_gain_grad, (1,))
    return (
        latents_out[:, None],
        pixel_grad,
        new_left,
        new_right,
        new_master,
        new_copy,
        kv_grad,
        new_kv,
        latent_grad,
        new_latent,
        in_gain_grad,
        new_in_gain,
        lat_gain_grad,
        new_lat_gains,
    )


def solution(mesh):
    pixel_spec = P(None, "img", "pix", None)
    slot_spec = P(("img", "pix"), None, None)
    in_specs = (
        (pixel_spec, P(), P()) + (slot_spec,) * 5 + (P(),) * 4 + (pixel_spec,)
    )
    out_specs = (pixel_spec, pixel_spec) + (slot_spec,) * 4 + (P(),) * 8
    return jax.shard_map(shards, mesh=mesh, in_specs=in_specs, out_specs=out_specs, check_vma=False)
```

profile of v0, /device:TPU:0, one launch (start us, length us, event | category | flops | bytes accessed | tf_op | source)
XLA Modules:
  0.0 669.0 jit_solution(5432599502976371848)
XLA Ops:
  14.1 22.2 %prepare_pixels.1.feat_ref = bf16[2,264,10368]{2,1,0:T(8,128)(2,1)} custom-call(s32[3]{0:T(128)} %pad_add_fusion.place_ref, f32[2,261,1,10368]{3,2,1,0:T(1,128)} %bitcast.122, f32[261,1]{1,0:T(8,128)} %broadcast_in_dim.120.gain_ref), custom_call_target="tpu_custom_call" | custom-call | bytes 32845824 | tf_op jit(solution)/shard_map/prepare_pixels/pallas_call | solution.py:113
  37.7 53.7 %all-gather.2.cloned.1.call-done.blocks_ref = bf16[256,128,128]{2,1,0:T(8,128)(2,1)} async-done(((bf16[8,128,128]{2,1,0:T(8,128)(2,1)}), bf16[256,128,128]{2,1,0:T(8,128)(2,1)}) %all-gather.2.cloned.1.call-update) | async-done | bytes 8388624 | tf_op jit(solution)/shard_map/all_gather | solution.py:473
  91.4 195.7 %make_query.1 = (bf16[512,1024]{1,0:T(8,128)(2,1)}, bf16[512,1024]{1,0:T(8,128)(2,1)}, bf16[264,512]{1,0:T(8,128)(2,1)}, bf16[1024,1024]{1,0:T(8,128)(2,1)}, bf1...) custom-call(s32[256]{0:T(256)} %owner_ref.1, ...), custom_call_target="tpu_custom_call" | custom-call | flops 1610612736 | bytes 16777216 | tf_op jit(solution)/shard_map/make_query/pallas_call | solution.py:275
  287.1 28.2 %attend.1 = (bf16[2,10368,512]{2,1,0:T(8,128)(2,1)}, bf16[2,264,512]{2,1,0:T(8,128)(2,1)}) custom-call(bf16[2,264,10368]{2,1,0:T(8,128)(2,1)} %prepare_pixels.1.feat_ref, bf16[264,512]{1,0:T(8,128)(2,1)} %get-tuple-element.35.query_ref.qc_ref), custom_call_target="tpu_custom_call" | custom-call | flops 22422749184 | bytes 42467328 | tf_op jit(solution)/shard_map/attend/pallas_call | solution.py:152
  320.0 4.2 all-to-all-start
  325.5 14.2 %all-to-all-done = bf16[8,264,128]{2,1,0:T(8,128)(2,1)} async-done(((bf16[8,264,128]{2,1,0:T(8,128)(2,1)}), bf16[8,264,128]{2,1,0:T(8,128)(2,1)}, u32[]{:S(2)}, u32[]{:S(2)}) %all-to-all-start) | async-done | bytes 540704 | tf_op jit(solution)/shard_map/all_to_all | solution.py:394
  353.7 3.8 all-to-all-start.1
  366.1 8.0 %slot_grads.1 = (bf16[128,128,128]{2,1,0:T(8,128)(2,1)}, bf16[128,128,128]{2,1,0:T(8,128)(2,1)}) custom-call(s32[256]{0:T(256)} %fusion.58.where_ref, bf16[3,128,1024]{2,1,0:T(8,128)(2,1)} %get-tuple-element.173.left_ref, bf16[3,128,1024]{2,1,0:T(8,128)(2,1)} %get-tuple-element.174.right_ref), custom_call_target="tpu_custom_call" | custom-call | tf_op jit(solution)/shard_map/slot_grads/pallas_call | solution.py:325
  375.1 4.1 all-to-all-start.9
  383.8 33.5 %attend_back.2 = (f32[2,261,1,10368]{3,2,1,0:T(1,128)}, f32[264,512]{1,0:T(8,128)}, f32[261,1]{1,0:T(8,128)}) custom-call(f32[2,261,1,10368]{3,2,1,0:T(1,128)} %bitcast.123, bf16[2,264,10368]{2,1,0:T(8,128)(2,1)} %prepare_pixels.1.feat_ref, bf16[2,10368,512]{2,1,0:T(8,128)(2,1)} %get-tuple-element.40.exp_ref, f32[261,1]{1,0:T(8,128)} %broadcast_in_dim.120.gain_ref, ...), custom_call_target="tpu_custom_call" | custom-call | flops 22422749184 | bytes 41472000 | tf_op jit(solution)/shard_map/attend_back/pallas_call | solution.py:213
  417.3 33.7 %attend_back.3 = (f32[2,261,1,10368]{3,2,1,0:T(1,128)}, f32[264,512]{1,0:T(8,128)}, f32[261,1]{1,0:T(8,128)}) custom-call(f32[2,261,1,10368]{3,2,1,0:T(1,128)} %bitcast.124, bf16[2,264,10368]{2,1,0:T(8,128)(2,1)} %prepare_pixels.1.feat_ref, bf16[2,10368,512]{2,1,0:T(8,128)(2,1)} %get-tuple-element.40.exp_ref, ...), custom_call_target="tpu_custom_call", output_to_operand_aliasing={{0}: (6, {})} | custom-call | flops 22422749184 | bytes 41472000 | tf_op jit(solution)/shard_map/attend_back/pallas_call | solution.py:213
  454.2 6.0 all-to-all-start.2
  462.8 8.3 %all-to-all-done.2 = bf16[8,33,512]{2,1,0:T(8,128)(2,1)S(1)} async-done(((bf16[8,33,512]{2,1,0:T(8,128)(2,1)}), bf16[8,33,512]{2,1,0:T(8,128)(2,1)S(1)}, u32[]{:S(2)}, u32[]{:S(2)}) %all-to-all-start.2) | async-done | bytes 270368 | tf_op jit(solution)/shard_map/all_to_all | solution.py:394
  471.8 3.8 all-to-all-start.6
  476.6 16.3 %all-to-all-done.6 = bf16[8,33,1024]{2,1,0:T(8,128)(2,1)S(1)} async-done(((bf16[8,33,1024]{2,1,0:T(8,128)(2,1)}), bf16[8,33,1024]{2,1,0:T(8,128)(2,1)S(1)}, u32[]{:S(2)}, u32[]{:S(2)}) %all-to-all-start.6) | async-done | bytes 540704 | tf_op jit(solution)/shard_map/all_to_all | solution.py:394
  493.7 4.1 all-to-all-start.3
  497.9 6.7 all-to-all-done.3
  505.5 3.5 all-to-all-start.7
  510.0 9.2 %all-to-all-done.7 = f32[4,33,1024]{2,1,0:T(8,128)S(1)} async-done(((f32[4,33,1024]{2,1,0:T(8,128)}), f32[4,33,1024]{2,1,0:T(8,128)S(1)}, u32[]{:S(2)}, u32[]{:S(2)}) %all-to-all-start.7) | async-done | bytes 540704 | tf_op jit(solution)/shard_map/all_to_all | solution.py:394
  519.9 4.1 all-to-all-start.4
  525.2 9.1 %all-to-all-done.4 = bf16[8,33,512]{2,1,0:T(8,128)(2,1)} async-done(((bf16[8,33,512]{2,1,0:T(8,128)(2,1)}), bf16[8,33,512]{2,1,0:T(8,128)(2,1)}, u32[]{:S(2)}, u32[]{:S(2)}) %all-to-all-start.4) | async-done | bytes 270368 | tf_op jit(solution)/shard_map/all_to_all | solution.py:394
  535.4 4.2 all-to-all-start.10
  539.6 4.6 add_convert_fusion.1
  552.7 12.0 %all-to-all-done.10 = bf16[8,64,1024]{2,1,0:T(8,128)(2,1)} async-done(((bf16[8,64,1024]{2,1,0:T(8,128)(2,1)}), bf16[8,64,1024]{2,1,0:T(8,128)(2,1)}, u32[]{:S(2)}, u32[]{:S(2)}) %all-to-all-start.10) | async-done | bytes 1048608 | tf_op jit(solution)/shard_map/all_to_all | solution.py:394
  565.6 4.2 all-to-all-start.8
  569.9 4.9 multiply_reduce_fusion.1
  574.8 15.9 %collective-permute-done.1 = bf16[64,128,128]{2,1,0:T(8,128)(2,1)} collective-permute-done((bf16[64,128,128]{2,1,0:T(8,128)(2,1)}, bf16[64,128,128]{2,1,0:T(8,128)(2,1)}, u32[]{:S(2)}, u32[]{:S(2)}) %collective-permute-start.1) | collective-permute-done | bytes 2097184 | tf_op jit(solution)/shard_map/ppermute | solution.py:525
  590.7 4.8 add_convert_fusion
  595.5 6.0 all-to-all-start.5
  605.7 3.5 multiply_reduce_fusion.2
  624.0 23.6 %all-to-all-done.5 = bf16[64,128,128]{2,1,0:T(8,128)(2,1)} async-done(((bf16[64,128,128]{2,1,0:T(8,128)(2,1)}), bf16[64,128,128]{2,1,0:T(8,128)(2,1)}, u32[]{:S(2)}, u32[]{:S(2)}) %all-to-all-start.5) | async-done | bytes 2097184 | tf_op jit(solution)/shard_map/all_to_all | solution.py:394
  650.4 11.3 %update_slots.1 = (f32[8,128,128]{2,1,0:T(8,128)}, f32[8,128,128]{2,1,0:T(8,128)}, f32[8,128,128]{2,1,0:T(8,128)}, bf16[8,128,128]{2,1,0:T(8,128)(2,1)}) custom-call(s32[8]{0:T(128)} %select_reduce_fusion.block_ref, bf16[512,1024]{1,0:T(8,128)(2,1)} %get-tuple-element.43.lat_ref, bf16[512,1024]{1,0:T(8,128)(2,1)} %multiply_convert_fusion.dq_ref, ...), custom_call_target="tpu_custom_call" | custom-call | tf_op jit(solution)/shard_map/update_slots/pallas_call | solution.py:376
  (186 shorter events, 85.1 us)
Async XLA Ops:
  7.2 84.2 %all-gather.2.cloned.1.call-start = ((), (), s32[]{:S(2)}) async-start(), calls=%async_computation.11 | async-start | bytes 8650752 | tf_op jit(solution)/shard_map/all_gather | solution.py:473
  13.4 23.5 %copy-start.3 = (bf16[2,261,1024]{2,1,0:T(8,128)(2,1)}, bf16[2,261,1024]{2,1,0:T(8,128)(2,1)S(1)}, u32[]{:S(2)}) copy-start(bf16[2,261,1024]{2,1,0:T(8,128)(2,1)S(1)} %copy.123) | copy-start | bytes 3207172
  14.1 22.2 %copy-start.30 = (f32[2,1024]{1,0:T(2,128)S(1)}, f32[2,1024]{1,0:T(2,128)}, u32[]{:S(2)}) copy-start(f32[2,1024]{1,0:T(2,128)} %param.24) | copy-start | bytes 24580
  316.7 8.2 %copy-start = (f32[512,1024]{1,0:T(8,128)S(1)}, f32[512,1024]{1,0:T(8,128)}, u32[]{:S(2)}) copy-start(f32[512,1024]{1,0:T(8,128)} %lat_ref.1) | copy-start | bytes 6291460
  317.6 23.8 %copy-start.4 = (bf16[2,261,1024]{2,1,0:T(8,128)(2,1)S(1)}, bf16[2,261,1024]{2,1,0:T(8,128)(2,1)}, u32[]{:S(2)}) copy-start(bf16[2,261,1024]{2,1,0:T(8,128)(2,1)} %copy-done.3) | copy-start | bytes 3207172
  320.0 19.7 %all-to-all-start = ((bf16[8,264,128]{2,1,0:T(8,128)(2,1)}), bf16[8,264,128]{2,1,0:T(8,128)(2,1)}, u32[]{:S(2)}, u32[]{:S(2)}) async-start(bf16[8,264,128]{2,1,0:T(8,128)(2,1)} %copy.101), calls=%async_computation | async-start | bytes 1081344 | tf_op jit(solution)/shard_map/all_to_all | solution.py:394
  340.8 2.8 copy-start.15
  345.3 2.7 copy-start.27
  345.3 2.7 copy-start.28
  350.2 2.5 copy-start.37
  351.3 12.3 %copy-start.18 = (bf16[2,64,1024]{2,1,0:T(8,128)(2,1)S(1)}, bf16[2,64,1024]{2,1,0:T(8,128)(2,1)}, u32[]{:S(2)}) copy-start(bf16[2,64,1024]{2,1,0:T(8,128)(2,1)} %copy-done.17) | copy-start | bytes 786436
  353.7 20.4 %all-to-all-start.1 = ((bf16[8,264,128]{2,1,0:T(8,128)(2,1)}), bf16[8,264,128]{2,1,0:T(8,128)(2,1)S(1)}, u32[]{:S(2)}, u32[]{:S(2)}) async-start(bf16[8,264,128]{2,1,0:T(8,128)(2,1)} %broadcast_in_dim.57), calls=%async_computation.1 | async-start | bytes 1081344 | tf_op jit(solution)/shard_map/all_to_all | solution.py:394
  374.0 165.6 %collective-permute-start = (bf16[128,128,128]{2,1,0:T(8,128)(2,1)}, bf16[128,128,128]{2,1,0:T(8,128)(2,1)}, u32[]{:S(2)}, u32[]{:S(2)}) collective-permute-start(bf16[128,128,128]{2,1,0:T(8,128)(2,1)} %get-tuple-element.49), channel_id=1, source_target_pairs={{0,8},{8,0},{16,24},{24,16},{1,9},{9,1},{17,25},{25,17},{2,10},{10... | collective-permute-start | bytes 12582920 | tf_op jit(solution)/shard_map/ppermute | solution.py:516
  375.1 79.1 %all-to-all-start.9 = ((bf16[4,64,1024]{2,1,0:T(8,128)(2,1)}), bf16[4,64,1024]{2,1,0:T(8,128)(2,1)}, u32[]{:S(2)}, u32[]{:S(2)}) async-start(bf16[4,64,1024]{2,1,0:T(8,128)(2,1)} %broadcast_in_dim.116), calls=%async_computation.9 | async-start | bytes 1048576 | tf_op jit(solution)/shard_map/all_to_all | solution.py:394
  417.3 33.7 %copy-start.26 = (f32[261,1]{1,0:T(8,128)S(1)}, f32[261,1]{1,0:T(8,128)}, u32[]{:S(2)}) copy-start(f32[261,1]{1,0:T(8,128)} %get-tuple-element.46) | copy-start | bytes 3136
  417.3 34.8 %copy-start.23 = (f32[264,512]{1,0:T(8,128)S(1)}, f32[264,512]{1,0:T(8,128)}, u32[]{:S(2)}) copy-start(f32[264,512]{1,0:T(8,128)} %get-tuple-element.44) | copy-start | bytes 1622020
  451.0 9.2 %copy-start.35 = (bf16[1024]{0:T(1024)(128)(2,1)S(1)}, bf16[1024]{0:T(1024)(128)(2,1)}, u32[]{:S(2)}) copy-start(bf16[1024]{0:T(1024)(128)(2,1)} %get-tuple-element.142) | copy-start | bytes 6148
  451.0 9.2 %copy-start.16 = (f32[264,128]{1,0:T(8,128)S(1)}, f32[264,128]{1,0:T(8,128)}, u32[]{:S(2)}) copy-start(f32[264,128]{1,0:T(8,128)} %copy-done.15) | copy-start | bytes 405508
  454.2 16.9 %all-to-all-start.2 = ((bf16[8,33,512]{2,1,0:T(8,128)(2,1)}), bf16[8,33,512]{2,1,0:T(8,128)(2,1)S(1)}, u32[]{:S(2)}, u32[]{:S(2)}) async-start(bf16[8,33,512]{2,1,0:T(8,128)(2,1)} %reshape.256), calls=%async_computation.2 | async-start | bytes 655360 | tf_op jit(solution)/shard_map/all_to_all | solution.py:394
  471.8 21.1 %all-to-all-start.6 = ((bf16[8,33,1024]{2,1,0:T(8,128)(2,1)}), bf16[8,33,1024]{2,1,0:T(8,128)(2,1)S(1)}, u32[]{:S(2)}, u32[]{:S(2)}) async-start(bf16[8,33,1024]{2,1,0:T(8,128)(2,1)} %reshape.258), calls=%async_computation.6 | async-start | bytes 1310720 | tf_op jit(solution)/shard_map/all_to_all | solution.py:394
  493.7 10.9 %all-to-all-start.3 = ((f32[4,33,512]{2,1,0:T(8,128)}), f32[4,33,512]{2,1,0:T(8,128)}, u32[]{:S(2)}, u32[]{:S(2)}) async-start(f32[4,33,512]{2,1,0:T(8,128)} %broadcast_in_dim.60), calls=%async_computation.3 | async-start | bytes 655360 | tf_op jit(solution)/shard_map/all_to_all | solution.py:394
  505.5 13.7 %all-to-all-start.7 = ((f32[4,33,1024]{2,1,0:T(8,128)}), f32[4,33,1024]{2,1,0:T(8,128)S(1)}, u32[]{:S(2)}, u32[]{:S(2)}) async-start(f32[4,33,1024]{2,1,0:T(8,128)} %broadcast_in_dim.114), calls=%async_computation.7 | async-start | bytes 1310720 | tf_op jit(solution)/shard_map/all_to_all | solution.py:394
  519.9 14.4 %all-to-all-start.4 = ((bf16[8,33,512]{2,1,0:T(8,128)(2,1)}), bf16[8,33,512]{2,1,0:T(8,128)(2,1)}, u32[]{:S(2)}, u32[]{:S(2)}) async-start(bf16[8,33,512]{2,1,0:T(8,128)(2,1)} %broadcast_in_dim.61), calls=%async_computation.4 | async-start | bytes 655360 | tf_op jit(solution)/shard_map/all_to_all | solution.py:394
  535.4 29.3 %all-to-all-start.10 = ((bf16[8,64,1024]{2,1,0:T(8,128)(2,1)}), bf16[8,64,1024]{2,1,0:T(8,128)(2,1)}, u32[]{:S(2)}, u32[]{:S(2)}) async-start(bf16[8,64,1024]{2,1,0:T(8,128)(2,1)} %broadcast_in_dim.117), calls=%async_computation.10 | async-start | bytes 2097152 | tf_op jit(solution)/shard_map/all_to_all | solution.py:394
  544.3 46.4 %collective-permute-start.1 = (bf16[64,128,128]{2,1,0:T(8,128)(2,1)}, bf16[64,128,128]{2,1,0:T(8,128)(2,1)}, u32[]{:S(2)}, u32[]{:S(2)}) collective-permute-start(bf16[64,128,128]{2,1,0:T(8,128)(2,1)} %add_convert_fusion.1), channel_id=1, source_target_pairs={{0,16},{8,24},{16,0},{24,8},{1,17},{9,25},{17,1},{25,9},{2,18},{10... | collective-permute-start | bytes 6291464 | tf_op jit(solution)/shard_map/ppermute | solution.py:525
  551.0 18.8 %copy-start.29 = (f32[1,1024]{1,0:T(1,128)S(1)}, f32[1,1024]{1,0:T(1,128)}, u32[]{:S(2)}) copy-start(f32[1,1024]{1,0:T(1,128)} %get-tuple-element.163.gain_ref) | copy-start | bytes 12292
  565.6 29.9 %all-to-all-start.8 = ((bf16[8,33,1024]{2,1,0:T(8,128)(2,1)}), bf16[8,33,1024]{2,1,0:T(8,128)(2,1)}, u32[]{:S(2)}, u32[]{:S(2)}) async-start(bf16[8,33,1024]{2,1,0:T(8,128)(2,1)} %broadcast_in_dim.115), calls=%async_computation.8 | async-start | bytes 1310720 | tf_op jit(solution)/shard_map/all_to_all | solution.py:394
  569.8 35.3 %copy-start.33 = (f32[261]{0:T(512)}, f32[261]{0:T(512)S(1)}, u32[]{:S(2)}) copy-start(f32[261]{0:T(512)S(1)} %fusion.54) | copy-start | bytes 3136
  569.9 20.8 %copy-start.2 = (bf16[128,128,128]{2,1,0:T(8,128)(2,1)S(1)}, bf16[128,128,128]{2,1,0:T(8,128)(2,1)}, u32[]{:S(2)}) copy-start(bf16[128,128,128]{2,1,0:T(8,128)(2,1)} %get-tuple-element.48) | copy-start | bytes 12582916
  595.5 52.2 %all-to-all-start.5 = ((bf16[64,128,128]{2,1,0:T(8,128)(2,1)}), bf16[64,128,128]{2,1,0:T(8,128)(2,1)}, u32[]{:S(2)}, u32[]{:S(2)}) async-start(bf16[64,128,128]{2,1,0:T(8,128)(2,1)} %add_convert_fusion), calls=%async_computation.5 | async-start | bytes 4194304 | tf_op jit(solution)/shard_map/all_to_all | solution.py:394
  620.2 3.1 copy-start.31
  623.3 38.4 %copy-start.32 = (f32[2,1024]{1,0:T(2,128)}, f32[2,1024]{1,0:T(2,128)S(1)}, u32[]{:S(2)}) copy-start(f32[2,1024]{1,0:T(2,128)S(1)} %get-tuple-element.147) | copy-start | bytes 24580
  (22 other events, 32.3 us)
Sparse Core Ops, SparseCore 0:
  11.5 79.8 all-gather.1
where the time goes:
time: 680 us; the launch traced here: 669 us
  Pallas kernels  333 us (49%)
  waiting for transfers between devices  169 us (25%)
  starting transfers between devices  48.9 us (7%)
  other arithmetic  44.9 us (7%)
  local copies, waits for them, and re-layouts  38.7 us (6%)
  matrix products  18.6 us (3%)
  between operations  16.7 us (2%)
    pallas_call x1, Pallas kernels, make_query(): pl.pallas_call(query_body, in_specs=[pl.BlockSpec(memory_space=pltpu.SMEM...  196 us
    all_to_all x11, waiting for transfers between devices, swap(): return lax.all_to_all(array, axis, 0, 0, tiled=True)  99.3 us
    pallas_call x2, Pallas kernels, attend_back(): pl.pallas_call(attend_back_body, grid=(rows_dev // rows,), in_specs=in_sp...  67.2 us
    all_gather x1, waiting for transfers between devices, shards(): lax.all_gather(master.astype(jnp.bfloat16), ('img', 'pix'), axis=0, tiled...  53.7 us
    all_to_all x11, starting transfers between devices, swap(): return lax.all_to_all(array, axis, 0, 0, tiled=True)  48 us
    pallas_call x1, Pallas kernels, attend(): pl.pallas_call(attend_body, grid=(micro, rows_dev // rows), in_specs=[pl....  28.2 us
    pallas_call x1, Pallas kernels, prepare_pixels(): pl.pallas_call(prepare_body, grid=(micro, rows_dev // rows), in_specs=[pl...  22.2 us
    ppermute x1, waiting for transfers between devices, shards(): grads = grads + lax.ppermute(pieces[k], 'img', hop).astype(jnp.float32)  15.9 us
  transfers between devices with their start and end apart: 14, of which 10 were waited for; matrix products, arithmetic and copies ran while one was open for 11% of the time, Pallas kernels for 15%

commit v1 on v0

--- a/solution.py
+++ b/solution.py
@@ -170,6 +170,23 @@
     )(feats, query_cols)
 
 
+def tiles_of(feats):
+    rows_dev = feats.shape[2]
+    return rows_dev // tile_of(rows_dev, 1152)
+
+
+def parts_of(feats):
+    micro = feats.shape[0]
+    tiles = tiles_of(feats)
+    head = tiles - tiles // 2
+    parts = []
+    for m in range(micro):
+        parts.append((m, 0, head))
+        if head < tiles:
+            parts.append((m, head, tiles - head))
+    return parts
+
+
 def attend_back_body(pix_ref, feat_ref, exp_ref, gain_ref, dc_ref, qc_ref, *rest):
     grad_ref, score_ref, gain_sum_ref = rest[-3:]
     feats = feat_ref[0]
@@ -192,14 +209,13 @@
     grad_ref[0, :, 0, :] = (d_normed - level - normed * along) * scale
 
 
-def attend_back(micro_index, earlier, across, feats, weights, gain_column, d_cols, query_cols):
-    rows_dev = feats.shape[2]
-    rows = tile_of(rows_dev, 1152)
-    m = micro_index
+def attend_back(part, earlier, across, feats, weights, gain_column, d_cols, query_cols):
+    m, first, tiles = part
+    rows = feats.shape[2] // tiles_of(feats)
     in_specs = [
-        pl.BlockSpec((1, CIN, 1, rows), lambda t: (m, 0, 0, t)),
-        pl.BlockSpec((1, CEXT, rows), lambda t: (m, 0, t)),
-        pl.BlockSpec((1, rows, LAT), lambda t: (m, t, 0)),
+        pl.BlockSpec((1, CIN, 1, rows), lambda t: (m, 0, 0, first + t)),
+        pl.BlockSpec((1, CEXT, rows), lambda t: (m, 0, first + t)),
+        pl.BlockSpec((1, rows, LAT), lambda t: (m, first + t, 0)),
         pl.BlockSpec((CIN, 1), lambda t: (0, 0)),
         pl.BlockSpec((1, CEXT, LAT), lambda t: (m, 0, 0)),
         pl.BlockSpec((CEXT, LAT), lambda t: (0, 0)),
@@ -212,10 +228,10 @@
         operands.append(earlier)
     return pl.pallas_call(
         attend_back_body,
-        grid=(rows_dev // rows,),
+        grid=(tiles,),
         in_specs=in_specs,
         out_specs=[
-            pl.BlockSpec((1, CIN, 1, rows), lambda t: (m, 0, 0, t)),
+            pl.BlockSpec((1, CIN, 1, rows), lambda t: (m, 0, 0, first + t)),
             pl.BlockSpec((CEXT, LAT), lambda t: (0, 0)),
             pl.BlockSpec((CIN, 1), lambda t: (0, 0)),
         ],
@@ -225,46 +241,43 @@
             jax.ShapeDtypeStruct((CIN, 1), jnp.float32),
         ],
         input_output_aliases=aliases,
-        cost_estimate=cost(16 * rows_dev * LAT * CEXT, rows_dev * 4000),
+        cost_estimate=cost(16 * tiles * rows * LAT * CEXT, tiles * rows * 4000),
         name="attend_back",
     )(*operands)
 
 
 def query_body(owner_ref, blocks_ref, lat_ref, gain_ref, key_ref, *rest):
-    low_ref, query_ref, cols_ref, wq_ref, wo_ref, w1_ref, w2_ref, square_ref, sems = rest
+    low_ref, query_ref, cols_ref, wq_ref, wo_ref, w1_ref, w2_ref, sems = rest
+    squares = (wq_ref, wo_ref, w1_ref, w2_ref)
     side = DL // BLK
 
-    def fetch(matrix, target_ref):
+    def fetch(matrix):
         @pl.loop(0, PER_MATRIX)
         def _(block):
             row = pl.multiple_of((block // side) * BLK, BLK)
             column = pl.multiple_of((block % side) * BLK, BLK)
             pltpu.make_async_copy(
                 blocks_ref.at[owner_ref[matrix * PER_MATRIX + block]],
-                target_ref.at[pl.ds(row, BLK), pl.ds(column, BLK)],
+                squares[matrix].at[pl.ds(row, BLK), pl.ds(column, BLK)],
                 sems.at[matrix],
             ).start()
 
-    def settle(matrix, target_ref):
-        pltpu.make_async_copy(target_ref, target_ref, sems.at[matrix]).wait()
-
-    fetch(0, square_ref)
-    for matrix, target_ref in ((1, wo_ref), (2, w1_ref), (3, w2_ref)):
-        fetch(matrix, target_ref)
+    def settle(matrix):
+        pltpu.make_async_copy(squares[matrix], squares[matrix], sems.at[matrix]).wait()
+
+    for matrix in range(4):
+        fetch(matrix)
     lat_low = (standardize(lat_ref[...]) * gain_ref[...]).astype(jnp.bfloat16)
     low_ref[...] = lat_low
-    settle(0, square_ref)
-    keep = pltpu.make_async_copy(square_ref, wq_ref, sems.at[0])
-    keep.start()
-    query = dot(lat_low, square_ref[...]).astype(jnp.bfloat16)
+    settle(0)
+    query = dot(lat_low, wq_ref[...]).astype(jnp.bfloat16)
     query_ref[...] = query
     scores = dot_last(key_ref[...], query) * (1.0 / math.sqrt(DL))
     row = lax.broadcasted_iota(jnp.int32, (CEXT - CIN, LAT), 0) + CIN
     tail = jnp.where(row == MASK_ROW, 1.0, 0.0)
     cols_ref[...] = jnp.concatenate([scores, tail], axis=0).astype(jnp.bfloat16)
-    keep.wait()
-    for matrix, target_ref in ((1, wo_ref), (2, w1_ref), (3, w2_ref)):
-        settle(matrix, target_ref)
+    for matrix in range(1, 4):
+        settle(matrix)
 
 
 def make_query(owner, gathered, latent_array, gain, w_key):
@@ -275,37 +288,44 @@
     return pl.pallas_call(
         query_body,
         in_specs=[pl.BlockSpec(memory_space=pltpu.SMEM), hbm, vmem, vmem, vmem],
-        out_specs=[vmem] * 3 + [hbm] * 4,
+        out_specs=[vmem] * 7,
         out_shape=[rows, rows, jax.ShapeDtypeStruct((CEXT, LAT), jnp.bfloat16)] + [square] * 4,
-        scratch_shapes=[pltpu.VMEM((DL, DL), jnp.bfloat16), pltpu.SemaphoreType.DMA((4,))],
+        scratch_shapes=[pltpu.SemaphoreType.DMA((4,))],
         cost_estimate=cost(3 * LAT * DL * DL, 4 * NBLK * BLK * BLK),
         name="make_query",
     )(owner, gathered, latent_array, gain[None], w_key)
 
 
-def slot_grads_body(where_ref, left_ref, right_ref, keep_ref, send_ref, full_ref, zero_ref, sems):
-    half = NBLK // 2
+def image_sums_body(where_ref, *rest):
+    n_img = len(rest) - 7
+    pieces, (grads_ref, value_ref, resid_ref, rows_ref, full_ref, zero_ref, sems) = (
+        rest[:n_img],
+        rest[n_img:],
+    )
     side = DL // BLK
+    count = pieces[0].shape[1]
 
     def put(source, block):
-        place = where_ref[block]
-
-        @pl.when(place < half)
+        place = where_ref[n_img + block]
+
+        @pl.when(place >= 0)
         def _():
-            pltpu.make_async_copy(source, keep_ref.at[place], sems.at[0]).start()
-
-        @pl.when(place >= half)
-        def _():
-            pltpu.make_async_copy(source, send_ref.at[place - half], sems.at[1]).start()
-
+            pltpu.make_async_copy(source, grads_ref.at[place], sems.at[1]).start()
+
+    for piece in range(n_img):
+        first = pl.multiple_of(where_ref[piece] * count, count)
+        pltpu.make_async_copy(
+            pieces[piece], rows_ref.at[:, pl.ds(first, count), :], sems.at[0]
+        ).start()
     zero_ref[...] = jnp.zeros_like(zero_ref)
 
     @pl.loop(0, PER_MATRIX)
     def _(block):
         put(zero_ref, block)
 
+    pltpu.make_async_copy(rows_ref, rows_ref, sems.at[0]).wait()
     for matrix in range(3):
-        full_ref[matrix] = contract_rows(left_ref[matrix], right_ref[matrix]).astype(jnp.bfloat16)
+        full_ref[matrix] = contract_rows(rows_ref[matrix], rows_ref[3 + matrix]).astype(jnp.bfloat16)
 
         @pl.loop(0, PER_MATRIX)
         def _(block, matrix=matrix):
@@ -316,28 +336,38 @@
                 (matrix + 1) * PER_MATRIX + block,
             )
 
-    pltpu.make_async_copy(keep_ref, keep_ref, sems.at[0]).wait()
-    pltpu.make_async_copy(send_ref, send_ref, sems.at[1]).wait()
-
-
-def slot_grads(where, left_rows, right_rows):
-    half = jax.ShapeDtypeStruct((NBLK // 2, BLK, BLK), jnp.bfloat16)
+    value_ref[...] = contract_rows(rows_ref[7, :, :CEXT], rows_ref[6]).astype(jnp.bfloat16)
+    each = resid_ref.shape[0]
+    total = rows_ref[3, :each, :].astype(jnp.float32)
+    for first in range(each, rows_ref.shape[1], each):
+        total = total + rows_ref[3, first : first + each, :].astype(jnp.float32)
+    resid_ref[...] = total.astype(jnp.bfloat16)
+    pltpu.make_async_copy(grads_ref, grads_ref, sems.at[1]).wait()
+
+
+def image_sums(where, pieces, lat_rows):
+    n_img = len(pieces)
+    slabs, count, _ = pieces[0].shape
+    hbm = pl.BlockSpec(memory_space=pl.ANY)
+    vmem = pl.BlockSpec(memory_space=pltpu.VMEM)
     return pl.pallas_call(
-        slot_grads_body,
-        in_specs=[
-            pl.BlockSpec(memory_space=pltpu.SMEM),
-            pl.BlockSpec(memory_space=pltpu.VMEM),
-            pl.BlockSpec(memory_space=pltpu.VMEM),
-        ],
-        out_specs=[pl.BlockSpec(memory_space=pl.ANY)] * 2,
-        out_shape=[half, half],
+        image_sums_body,
+        in_specs=[pl.BlockSpec(memory_space=pltpu.SMEM)] + [hbm] * n_img,
+        out_specs=[hbm, vmem, vmem],
+        out_shape=[
+            jax.ShapeDtypeStruct((NBLK // n_img, BLK, BLK), jnp.bfloat16),
+            jax.ShapeDtypeStruct((CEXT, DL), jnp.bfloat16),
+            jax.ShapeDtypeStruct((lat_rows, DL), jnp.bfloat16),
+        ],
         scratch_shapes=[
+            pltpu.VMEM((slabs, n_img * count, DL), jnp.bfloat16),
             pltpu.VMEM((3, DL, DL), jnp.bfloat16),
             pltpu.VMEM((BLK, BLK), jnp.bfloat16),
             pltpu.SemaphoreType.DMA((2,)),
         ],
-        name="slot_grads",
-    )(where, left_rows, right_rows)
+        cost_estimate=cost(8 * n_img * count * DL * DL, 16 * DL * DL),
+        name="image_sums",
+    )(where, *pieces)
 
 
 def update_body(block_ref, lat_ref, dq_ref, sum_ref, ls_ref, rs_ref, lr_ref, rr_ref, ma_ref, *outs):
@@ -398,6 +428,49 @@
     return swap(jnp.broadcast_to(array[None], (lax.axis_size(axis), *array.shape)), axis)
 
 
+def near_hop(array, axis):
+    size = lax.axis_size(axis)
+    return lax.ppermute(array, axis, [(i, i ^ 1) for i in range(size)])
+
+
+def far_hop(array, axis, step):
+    size = lax.axis_size(axis)
+    return lax.ppermute(array, axis, [(i, (i + 2 * step) % size) for i in range(size)])
+
+
+def split_near(array, axis):
+    size = lax.axis_size(axis)
+    near = lax.axis_index(axis) % 2
+    pairs = array.reshape(size // 2, 2, *array.shape[1:])
+    return (
+        lax.dynamic_index_in_dim(pairs, near, 1, False),
+        lax.dynamic_index_in_dim(pairs, 1 - near, 1, False),
+    )
+
+
+def sum_parts(kept, sent, axis):
+    size = lax.axis_size(axis)
+    far = lax.axis_index(axis) // 2
+    got = near_hop(sent, axis)
+    kept = (kept.astype(jnp.float32) + got.astype(jnp.float32)).astype(jnp.bfloat16)
+    total = lax.dynamic_index_in_dim(kept, far, 0, False).astype(jnp.float32)
+    for step in range(1, size // 2):
+        part = lax.dynamic_index_in_dim(kept, (far + step) % (size // 2), 0, False)
+        total = total + far_hop(part, axis, step).astype(jnp.float32)
+    return total
+
+
+def gather_parts(array, axis):
+    size = lax.axis_size(axis)
+    near = lax.axis_index(axis) % 2
+    far = lax.axis_index(axis) // 2
+    got = [array] + [far_hop(array, axis, step) for step in range(1, size // 2)]
+    got = lax.dynamic_slice_in_dim(jnp.stack(got[::-1] * 2), size // 2 - 1 - far, size // 2, 0)
+    other = near_hop(got, axis)
+    both = jnp.where(near == 0, jnp.stack([got, other], axis=1), jnp.stack([other, got], axis=1))
+    return both.reshape(size, *array.shape)
+
+
 def total_of(partial):
     rows, width = partial.shape
     n_pix = lax.axis_size("pix")
@@ -406,10 +479,6 @@
     part = jnp.sum(swap(padded.reshape(n_pix, each, width), "pix").astype(jnp.float32), axis=0)
     part = jnp.sum(everyone(part, "img"), axis=0).astype(jnp.bfloat16)
     return everyone(part, "pix").reshape(n_pix * each, width)[:rows]
-
-
-def add_low(left_side, right_side):
-    return (left_side.astype(jnp.float32) + right_side.astype(jnp.float32)).astype(jnp.bfloat16)
 
 
 def latent_pass(numerator, denominator, lat_part, cot_rows, lat_gain, w_out, w_up, w_down):
@@ -431,16 +500,9 @@
     d_attended = product("mre,de->mrd", d_branch, w_out)
     d_numer = d_attended / denominator[..., None]
     d_denom = -jnp.sum(d_attended * numerator / (denominator * denominator)[..., None], axis=-1)
-    left_rows = jnp.stack([att_low, hn_low, act_low]).reshape(3, -1, DL)
-    right_rows = jnp.stack([d_branch, d_hidden, g_mlp]).reshape(3, -1, DL)
     gain_mlp = jnp.sum(d_normed * normed, axis=(0, 1))
-    lat_resid = jnp.sum(d_resid, axis=0)
-    return (
-        latents_out,
-        d_numer.astype(jnp.bfloat16),
-        d_denom,
-        (left_rows, right_rows, gain_mlp, lat_resid),
-    )
+    row_arrays = (att_low, hn_low, act_low, d_branch, d_hidden, g_mlp)
+    return (latents_out, d_numer.astype(jnp.bfloat16), d_denom, (row_arrays, gain_mlp))
 
 
 def shards(
@@ -498,7 +560,7 @@
         w_up,
         w_down,
     )
-    left_rows, right_rows, gain_mlp, lat_resid = latent_grads
+    row_arrays, gain_mlp = latent_grads
     d_numer = d_numer.reshape(micro * lat_rows, DL)
     head, rest = two_terms(d_denom.reshape(1, micro * lat_rows))
     d_cols = product("rd,cd->cr", d_numer, w_value).astype(jnp.bfloat16)
@@ -506,52 +568,72 @@
     d_cols = everyone(d_cols, "pix").reshape(n_pix, CEXT, micro, lat_rows)
     d_cols = d_cols.transpose(2, 1, 0, 3).reshape(micro, CEXT, LAT)
 
+    numer_rows = jnp.pad(numer_in.astype(jnp.bfloat16).T, ((0, 0), (0, DL - CIN)))
+    own = jnp.stack(
+        [array.reshape(micro * lat_rows, DL) for array in row_arrays] + [d_numer, numer_rows]
+    )
+    mate = [(i, i ^ 1) for i in range(n_img)]
+    pieces = [own, lax.ppermute(own, "img", mate)]
+    images = [img, img ^ 1]
+    far = []
+    for step in range(1, n_img // 2):
+        hop = [(i, (i + 2 * step) % n_img) for i in range(n_img)]
+        far.append(lax.ppermute(own, "img", hop))
+        images += [(img - 2 * step) % n_img, (img - 2 * step) % n_img ^ 1]
     device_of = owner // slots_dev
-    img_of = device_of // n_pix
-    n_far = n_img // 2
-    far_step = (img_of // 2 - img // 2) % n_far
-    where = (far_step * n_pix + device_of % n_pix) * slots_dev + owner % slots_dev
-    where = where + jnp.where(img_of % 2 == img % 2, 0, NBLK // 2)
-    keep, send = slot_grads(where.astype(jnp.int32), left_rows, right_rows)
-    got = lax.ppermute(send, "img", [(i, i ^ 1) for i in range(n_img)])
-    count = NBLK // 2 // n_far
-    pieces = [
-        add_low(keep[k * count : (k + 1) * count], got[k * count : (k + 1) * count])
-        for k in range(n_far)
-    ]
-    grads = pieces[0].astype(jnp.float32)
-    for k in range(1, n_far):
-        hop = [(i, (i + 2 * k) % n_img) for i in range(n_img)]
-        grads = grads + lax.ppermute(pieces[k], "img", hop).astype(jnp.float32)
-
-    value_grad = fine("cr,rd->cd", numer_in, d_numer)
-    early = jnp.concatenate([value_grad, gain_mlp[None]], axis=0)
+    place_of = device_of % n_pix * slots_dev + owner % slots_dev
+    where = jnp.where(device_of // n_pix == img, place_of, -1)
 
     results = (None,)
     score_sum = jnp.zeros((CEXT, LAT), jnp.float32)
     gain_sum = jnp.zeros((CIN, 1), jnp.float32)
-    for micro_index in range(micro):
+    width = DL // n_img
+    each = -(-CEXT // n_pix)
+    parts = parts_of(feats)
+    for at, part in enumerate(parts):
+        if at == len(parts) - 2:
+            far, gain_sum = lax.optimization_barrier((far, gain_sum))
+            for piece in far:
+                pieces += [piece, lax.ppermute(piece, "img", mate)]
+        if at == len(parts) - 1:
+            pieces, gain_sum = lax.optimization_barrier((pieces, gain_sum))
+            where = jnp.concatenate([jnp.stack(images), where]).astype(jnp.int32)
+            grads, value_part, resid_part = image_sums(where, pieces, lat_rows)
+            value_part = jnp.pad(value_part, ((0, each * n_pix - CEXT), (0, 0)))
+            value_part = lax.dynamic_slice_in_dim(value_part, img * width, width, 1)
+            value_sides = split_near(value_part.reshape(n_pix, each, width), "pix")
+            grad_sides = split_near(grads.reshape(n_pix, slots_dev, BLK, BLK), "pix")
+            gain_column, value_sides, grad_sides = lax.optimization_barrier(
+                (gain_column, value_sides, grad_sides)
+            )
         results = attend_back(
-            micro_index, results[0], across, feats, weights, gain_column, d_cols, query_cols
+            part, results[0], across, feats, weights, gain_column, d_cols, query_cols
         )
         score_sum = score_sum + results[1]
         gain_sum = gain_sum + results[2]
     pixel_grad = jnp.swapaxes(results[0].reshape(micro, 1, CIN, rows_dev), 2, 3)
 
-    early_total = total_of(early).astype(jnp.float32)
-    value_total = early_total[:CIN]
-    gain_mlp_total = early_total[CIN]
-    lat_part = jnp.sum(everyone(lat_resid.astype(jnp.bfloat16), "img").astype(jnp.float32), axis=0)
-    resid_total = everyone(lat_part.astype(jnp.bfloat16), "pix").reshape(LAT, DL)
-
-    late = jnp.concatenate([score_sum[:CIN], jnp.pad(gain_sum.T, ((0, 0), (0, LAT - CIN)))], axis=0)
+    value_part = sum_parts(*value_sides, "pix").astype(jnp.bfloat16)
+    resid_part = lax.dynamic_slice_in_dim(resid_part, img * width, width, 1)
+    early = gather_parts(jnp.concatenate([value_part, resid_part], axis=0), "pix")
+    early = gather_parts(early, "img").transpose(1, 2, 0, 3).reshape(n_pix, each + lat_rows, DL)
+    value_total = early[:, :each].reshape(n_pix * each, DL)[:CIN].astype(jnp.float32)
+    resid_total = early[:, each:].reshape(LAT, DL)
+
+    late = jnp.concatenate(
+        [
+            score_sum[:CIN],
+            jnp.pad(gain_sum.T, ((0, 0), (0, LAT - CIN))),
+            gain_mlp.reshape(DL // LAT, LAT),
+        ],
+        axis=0,
+    )
     late_total = total_of(late)
     score_total = late_total[:CIN]
     in_gain_grad = late_total[CIN, :CIN].astype(jnp.float32)
-
-    grads = grads.astype(jnp.bfloat16).reshape(n_pix * slots_dev, BLK, BLK)
-    grads = swap(grads, "pix").reshape(n_pix, slots_dev, BLK, BLK)
-    grads = jnp.sum(grads.astype(jnp.float32), axis=0)
+    gain_mlp_total = late_total[CIN + 1 :].reshape(DL).astype(jnp.float32)
+
+    grads = sum_parts(*grad_sides, "pix")
 
     d_query = (contract_rows(score_total, w_key) * inv_root).astype(jnp.bfloat16)
     key_total = dot(score_total, query) * inv_root

time: 680 us -> 457 us (0.67)
  the two profiles are of different devices: /device:TPU:0 before, /device:TPU:11 now
where the time goes in v1:
time: 457 us; the launch traced here: 450 us
  Pallas kernels  159 us (35%)
  waiting for transfers between devices  106 us (23%)
  local copies, waits for them, and re-layouts  62 us (14%)
  starting transfers between devices  51.2 us (11%)
  other arithmetic  39.7 us (9%)
  between operations  16.5 us (4%)
  matrix products  15.1 us (3%)
    pallas_call x4, Pallas kernels, attend_back(): pl.pallas_call(attend_back_body, grid=(tiles,), in_specs=in_specs, out_sp...  73.7 us
    all_gather x1, waiting for transfers between devices, shards(): lax.all_gather(master.astype(jnp.bfloat16), ('img', 'pix'), axis=0, tiled...  52.4 us
    all_to_all x5, starting transfers between devices, swap(): return lax.all_to_all(array, axis, 0, 0, tiled=True)  31.1 us
    pallas_call x1, Pallas kernels, attend(): pl.pallas_call(attend_body, grid=(micro, rows_dev // rows), in_specs=[pl....  28.2 us
    pallas_call x1, Pallas kernels, prepare_pixels(): pl.pallas_call(prepare_body, grid=(micro, rows_dev // rows), in_specs=[pl...  22.2 us
    unnamed x102, local copies, waits for them, and re-layouts  20.1 us
    ppermute x10, waiting for transfers between devices, far_hop(): lax.ppermute(array, axis, [(i, (i + 2 * step) % size) for i in range(size)])  19.8 us
    ppermute x4, waiting for transfers between devices, near_hop(): return lax.ppermute(array, axis, [(i, i ^ 1) for i in range(size)])  19.2 us
  transfers between devices with their start and end apart: 23, of which 10 were waited for; matrix products, arithmetic and copies ran while one was open for 13% of the time, Pallas kernels for 24%

profile of v1, /device:TPU:11, one launch (start us, length us, event | category | flops | bytes accessed | tf_op | source)
XLA Modules:
  0.0 450.0 jit_solution(18350219787966955730)
XLA Ops:
  14.1 22.2 %prepare_pixels.1.feat_ref = bf16[2,264,10368]{2,1,0:T(8,128)(2,1)} custom-call(s32[3]{0:T(128)} %pad_add_fusion.place_ref, f32[2,261,1,10368]{3,2,1,0:T(1,128)} %bitcast.204, f32[261,1]{1,0:T(8,128)} %copy.142.gain_ref), custom_call_target="tpu_custom_call" | custom-call | bytes 32845824 | tf_op jit(solution)/shard_map/prepare_pixels/pallas_call | solution.py:113
  37.7 52.4 %all-gather.2.cloned.1.call-done.blocks_ref = bf16[256,128,128]{2,1,0:T(8,128)(2,1)} async-done(((bf16[8,128,128]{2,1,0:T(8,128)(2,1)}), bf16[256,128,128]{2,1,0:T(8,128)(2,1)}) %all-gather.2.cloned.1.call-update) | async-done | bytes 8388624 | tf_op jit(solution)/shard_map/all_gather | solution.py:535
  90.2 11.6 %make_query.1 = (bf16[512,1024]{1,0:T(8,128)(2,1)}, bf16[512,1024]{1,0:T(8,128)(2,1)}, bf16[264,512]{1,0:T(8,128)(2,1)}, bf16[1024,1024]{1,0:T(8,128)(2,1)}, bf1...) custom-call(s32[256]{0:T(256)} %owner_ref.1, ...), custom_call_target="tpu_custom_call" | custom-call | flops 1610612736 | bytes 16777216 | tf_op jit(solution)/shard_map/make_query/pallas_call | solution.py:288
  101.8 28.2 %attend.1 = (bf16[2,10368,512]{2,1,0:T(8,128)(2,1)}, bf16[2,264,512]{2,1,0:T(8,128)(2,1)}) custom-call(bf16[2,264,10368]{2,1,0:T(8,128)(2,1)} %prepare_pixels.1.feat_ref, bf16[264,512]{1,0:T(8,128)(2,1)} %get-tuple-element.54.query_ref.qc_ref), custom_call_target="tpu_custom_call" | custom-call | flops 22422749184 | bytes 42467328 | tf_op jit(solution)/shard_map/attend/pallas_call | solution.py:152
  132.4 2.3 copy.146
  134.7 4.9 %all-to-all-start = ((bf16[8,264,128]{2,1,0:T(8,128)(2,1)}), bf16[8,264,128]{2,1,0:T(8,128)(2,1)}, u32[]{:S(2)}, u32[]{:S(2)}) async-start(bf16[8,264,128]{2,1,0:T(8,128)(2,1)} %copy.146), calls=%async_computation | async-start | bytes 1081344 | tf_op jit(solution)/shard_map/all_to_all | solution.py:424
  141.5 10.4 %all-to-all-done = bf16[8,264,128]{2,1,0:T(8,128)(2,1)} async-done(((bf16[8,264,128]{2,1,0:T(8,128)(2,1)}), bf16[8,264,128]{2,1,0:T(8,128)(2,1)}, u32[]{:S(2)}, u32[]{:S(2)}) %all-to-all-start) | async-done | bytes 540704 | tf_op jit(solution)/shard_map/all_to_all | solution.py:424
  166.9 6.7 %all-to-all-start.1 = ((bf16[8,264,128]{2,1,0:T(8,128)(2,1)}), bf16[8,264,128]{2,1,0:T(8,128)(2,1)}, u32[]{:S(2)}, u32[]{:S(2)}) async-start(bf16[8,264,128]{2,1,0:T(8,128)(2,1)} %broadcast_in_dim.42), calls=%async_computation.1 | async-start | bytes 1081344 | tf_op jit(solution)/shard_map/all_to_all | solution.py:424
  190.3 20.1 %attend_back.4 = (f32[2,261,1,10368]{3,2,1,0:T(1,128)}, f32[264,512]{1,0:T(8,128)}, f32[261,1]{1,0:T(8,128)}) custom-call(f32[2,261,1,10368]{3,2,1,0:T(1,128)} %bitcast.205, bf16[2,264,10368]{2,1,0:T(8,128)(2,1)} %prepare_pixels.1.feat_ref, bf16[2,10368,512]{2,1,0:T(8,128)(2,1)} %get-tuple-element.59.exp_ref, f32[261,1]{1,0:T(8,128)} %copy.142.gain_ref, ...), custom_call_target="tpu_custom_call" | custom-call | flops 12457082880 | bytes 23040000 | tf_op jit(solution)/shard_map/attend_back/pallas_call | solution.py:229
  210.3 16.8 %attend_back.5 = (f32[2,261,1,10368]{3,2,1,0:T(1,128)}, f32[264,512]{1,0:T(8,128)}, f32[261,1]{1,0:T(8,128)}) custom-call(f32[2,261,1,10368]{3,2,1,0:T(1,128)} %bitcast.206, bf16[2,264,10368]{2,1,0:T(8,128)(2,1)} %prepare_pixels.1.feat_ref, bf16[2,10368,512]{2,1,0:T(8,128)(2,1)} %get-tuple-element.59.exp_ref, ...), custom_call_target="tpu_custom_call", output_to_operand_aliasing={{0}: (6, {})} | custom-call | flops 9965666304 | bytes 18432000 | tf_op jit(solution)/shard_map/attend_back/pallas_call | solution.py:229
  232.1 20.1 %attend_back.6 = (f32[2,261,1,10368]{3,2,1,0:T(1,128)}, f32[264,512]{1,0:T(8,128)}, f32[261,1]{1,0:T(8,128)}) custom-call(f32[2,261,1,10368]{3,2,1,0:T(1,128)} %bitcast.207, bf16[2,264,10368]{2,1,0:T(8,128)(2,1)} %prepare_pixels.1.feat_ref, bf16[2,10368,512]{2,1,0:T(8,128)(2,1)} %get-tuple-element.59.exp_ref, ...), custom_call_target="tpu_custom_call", output_to_operand_aliasing={{0}: (6, {})} | custom-call | flops 12457082880 | bytes 23040000 | tf_op jit(solution)/shard_map/attend_back/pallas_call | solution.py:229
  253.1 12.4 %image_sums.1 = (bf16[64,128,128]{2,1,0:T(8,128)(2,1)}, bf16[264,1024]{1,0:T(8,128)(2,1)}, bf16[64,1024]{1,0:T(8,128)(2,1)}) custom-call(s32[260]{0:T(512)} %concatenate.17.where_ref, bf16[8,128,1024]{2,1,0:T(8,128)(2,1)} %bitcast_dynamic-update-slice_fusion.rest_0_, bf16[8,128,1024]{2,1,0:T(8,128)(2,1)} %collective-permute-done.rest_1_, ...), custom_call_target="tpu_custom_call" | custom-call | flops 4294967296 | bytes 16777216 | tf_op jit(solution)/shard_map/image_sums/pallas_call | solution.py:353
  266.5 3.1 dynamic-slice_bitcast_fusion
  271.9 16.8 %attend_back.7 = (f32[2,261,1,10368]{3,2,1,0:T(1,128)}, f32[264,512]{1,0:T(8,128)}, f32[261,1]{1,0:T(8,128)}) custom-call(f32[2,261,1,10368]{3,2,1,0:T(1,128)} %bitcast.208, bf16[2,264,10368]{2,1,0:T(8,128)(2,1)} %prepare_pixels.1.feat_ref, bf16[2,10368,512]{2,1,0:T(8,128)(2,1)} %get-tuple-element.59.exp_ref, ...), custom_call_target="tpu_custom_call", output_to_operand_aliasing={{0}: (6, {})} | custom-call | flops 9965666304 | bytes 18432000 | tf_op jit(solution)/shard_map/attend_back/pallas_call | solution.py:229
  292.1 2.7 collective-permute-start.9
  298.1 7.3 %all-to-all-start.2 = ((bf16[8,33,512]{2,1,0:T(8,128)(2,1)}), bf16[8,33,512]{2,1,0:T(8,128)(2,1)}, u32[]{:S(2)}, u32[]{:S(2)}) async-start(bf16[8,33,512]{2,1,0:T(8,128)(2,1)} %convert_element_type.190), calls=%async_computation.2 | async-start | bytes 655360 | tf_op jit(solution)/shard_map/all_to_all | solution.py:424
  307.8 6.7 %collective-permute-done.12 = bf16[97,256]{1,0:T(8,128)(2,1)S(1)} collective-permute-done((bf16[97,256]{1,0:T(8,128)(2,1)S(1)}, bf16[97,256]{1,0:T(8,128)(2,1)S(1)}, u32[]{:S(2)}, u32[]{:S(2)}) %collective-permute-start.12) | collective-permute-done | bytes 49696 | tf_op jit(solution)/shard_map/ppermute | solution.py:438
  316.5 19.2 %collective-permute-done.14 = bf16[4,97,256]{2,1,0:T(8,128)(2,1)S(1)} collective-permute-done((bf16[4,97,256]{2,1,0:T(8,128)(2,1)}, bf16[4,97,256]{2,1,0:T(8,128)(2,1)S(1)}, u32[]{:S(2)}, u32[]{:S(2)}) %collective-permute-start.14) | collective-permute-done | bytes 198688 | tf_op jit(solution)/shard_map/ppermute | solution.py:433
  341.0 6.6 %all-to-all-start.3 = ((f32[4,33,512]{2,1,0:T(8,128)}), f32[4,33,512]{2,1,0:T(8,128)}, u32[]{:S(2)}, u32[]{:S(2)}) async-start(f32[4,33,512]{2,1,0:T(8,128)} %broadcast_in_dim.78), calls=%async_computation.3 | async-start | bytes 655360 | tf_op jit(solution)/shard_map/all_to_all | solution.py:424
  347.6 2.8 fusion.22
  350.6 2.9 all-to-all-done.3
  356.7 5.7 %all-to-all-start.4 = ((bf16[8,33,512]{2,1,0:T(8,128)(2,1)}), bf16[8,33,512]{2,1,0:T(8,128)(2,1)}, u32[]{:S(2)}, u32[]{:S(2)}) async-start(bf16[8,33,512]{2,1,0:T(8,128)(2,1)} %broadcast_in_dim.79), calls=%async_computation.4 | async-start | bytes 655360 | tf_op jit(solution)/shard_map/all_to_all | solution.py:424
  362.4 2.5 fusion.85
  364.9 2.4 fusion.28
  380.8 3.2 multiply_reduce_fusion.1
  387.4 8.9 %collective-permute-done.5 = bf16[8,128,128]{2,1,0:T(8,128)(2,1)} collective-permute-done((bf16[8,128,128]{2,1,0:T(8,128)(2,1)}, bf16[8,128,128]{2,1,0:T(8,128)(2,1)}, u32[]{:S(2)}, u32[]{:S(2)}) %collective-permute-start.5) | collective-permute-done | bytes 262176 | tf_op jit(solution)/shard_map/ppermute | solution.py:438
  396.3 2.4 collective-permute-done.6
  400.8 11.3 %update_slots.1 = (f32[8,128,128]{2,1,0:T(8,128)}, f32[8,128,128]{2,1,0:T(8,128)}, f32[8,128,128]{2,1,0:T(8,128)}, bf16[8,128,128]{2,1,0:T(8,128)(2,1)}) custom-call(s32[8]{0:T(128)} %select_reduce_fusion.block_ref, bf16[512,1024]{1,0:T(8,128)(2,1)} %get-tuple-element.76.lat_ref, bf16[512,1024]{1,0:T(8,128)(2,1)} %copy-done.23, ...), custom_call_target="tpu_custom_call" | custom-call | tf_op jit(solution)/shard_map/update_slots/pallas_call | solution.py:406
  416.3 4.1 reshape.283
  428.2 2.2 copy.164
  435.3 3.0 copy.168
  438.3 3.0 copy.169
  (241 shorter events, 108.8 us)
Async XLA Ops:
  7.2 83.0 %all-gather.2.cloned.1.call-start = ((), (), s32[]{:S(2)}) async-start(), calls=%async_computation.5 | async-start | bytes 8650752 | tf_op jit(solution)/shard_map/all_gather | solution.py:535
  13.5 23.5 %copy-start.6 = (bf16[2,261,1024]{2,1,0:T(8,128)(2,1)}, bf16[2,261,1024]{2,1,0:T(8,128)(2,1)S(1)}, u32[]{:S(2)}) copy-start(bf16[2,261,1024]{2,1,0:T(8,128)(2,1)S(1)} %copy.178) | copy-start | bytes 3207172
  14.1 22.2 %copy-start.32 = (f32[2,1024]{1,0:T(2,128)S(1)}, f32[2,1024]{1,0:T(2,128)}, u32[]{:S(2)}) copy-start(f32[2,1024]{1,0:T(2,128)} %param.24) | copy-start | bytes 24580
  132.4 23.1 %copy-start.7 = (bf16[2,261,1024]{2,1,0:T(8,128)(2,1)S(1)}, bf16[2,261,1024]{2,1,0:T(8,128)(2,1)}, u32[]{:S(2)}) copy-start(bf16[2,261,1024]{2,1,0:T(8,128)(2,1)} %copy-done.6) | copy-start | bytes 3207172
  134.7 17.1 %all-to-all-start = ((bf16[8,264,128]{2,1,0:T(8,128)(2,1)}), bf16[8,264,128]{2,1,0:T(8,128)(2,1)}, u32[]{:S(2)}, u32[]{:S(2)}) async-start(bf16[8,264,128]{2,1,0:T(8,128)(2,1)} %copy.146), calls=%async_computation | async-start | bytes 1081344 | tf_op jit(solution)/shard_map/all_to_all | solution.py:424
  166.9 18.8 %all-to-all-start.1 = ((bf16[8,264,128]{2,1,0:T(8,128)(2,1)}), bf16[8,264,128]{2,1,0:T(8,128)(2,1)}, u32[]{:S(2)}, u32[]{:S(2)}) async-start(bf16[8,264,128]{2,1,0:T(8,128)(2,1)} %broadcast_in_dim.42), calls=%async_computation.1 | async-start | bytes 1081344 | tf_op jit(solution)/shard_map/all_to_all | solution.py:424
  181.3 46.7 %collective-permute-start.1 = (bf16[8,128,1024]{2,1,0:T(8,128)(2,1)}, bf16[8,128,1024]{2,1,0:T(8,128)(2,1)}, u32[]{:S(2)}, u32[]{:S(2)}) collective-permute-start(bf16[8,128,1024]{2,1,0:T(8,128)(2,1)} %bitcast_dynamic-update-slice_fusion.rest_0_), channel_id=1, source_target_pairs={{0,16},{8,24},{16,0},{24,8},{1,17},{9,25},{17,1},{25,9},{2,18},{10... | collective-permute-start | bytes 6291464 | tf_op jit(solution)/shard_map/ppermute | solution.py:581
  182.5 70.6 %collective-permute-start = (bf16[8,128,1024]{2,1,0:T(8,128)(2,1)}, bf16[8,128,1024]{2,1,0:T(8,128)(2,1)}, u32[]{:S(2)}, u32[]{:S(2)}) collective-permute-start(bf16[8,128,1024]{2,1,0:T(8,128)(2,1)} %bitcast_dynamic-update-slice_fusion.rest_0_), channel_id=1, source_target_pairs={{0,8},{8,0},{16,24},{24,16},{1,9},{9,1},{17,25},{25,17},{2,10},{10... | collective-permute-start | bytes 6291464 | tf_op jit(solution)/shard_map/ppermute | solution.py:576
  210.3 16.8 %copy-start.29 = (f32[261,1]{1,0:T(8,128)S(1)}, f32[261,1]{1,0:T(8,128)}, u32[]{:S(2)}) copy-start(f32[261,1]{1,0:T(8,128)} %get-tuple-element.60) | copy-start | bytes 3136
  228.0 25.1 %collective-permute-start.2 = (bf16[8,128,1024]{2,1,0:T(8,128)(2,1)}, bf16[8,128,1024]{2,1,0:T(8,128)(2,1)}, u32[]{:S(2)}, u32[]{:S(2)}) collective-permute-start(bf16[8,128,1024]{2,1,0:T(8,128)(2,1)} %collective-permute-done.1.rest_2_), channel_id=1, source_target_pairs={{0,8},{8,0},{16,24},{24,16},{1,9},{9,1},{17,25},{25,17},{2,10},{10... | collective-permute-start | bytes 6291464 | tf_op jit(solution)/shard_map/ppermute | solution.py:597
  230.9 21.3 %copy-start.35 = (f32[512]{0:T(512)}, f32[512]{0:T(512)S(1)}, u32[]{:S(2)}) copy-start(f32[512]{0:T(512)S(1)} %multiply_reduce_fusion.4) | copy-start | bytes 6148
  270.5 20.0 %collective-permute-start.7 = (bf16[4,33,256]{2,1,0:T(8,128)(2,1)S(1)}, bf16[4,33,256]{2,1,0:T(8,128)(2,1)S(1)}, u32[]{:S(2)}, u32[]{:S(2)}) collective-permute-start(bf16[4,33,256]{2,1,0:T(8,128)(2,1)S(1)} %get-tuple-element.91), channel_id=1, source_target_pairs={{0,1},{1,0},{2,3},{3,2},{4,5},{5,4},{6,7},{7,6},{8,9},{9,8},{10,11... | collective-permute-start | bytes 202760 | tf_op jit(solution)/shard_map/ppermute | solution.py:433
  271.9 16.8 %copy-start.25 = (f32[264,512]{1,0:T(8,128)S(1)}, f32[264,512]{1,0:T(8,128)}, u32[]{:S(2)}) copy-start(f32[264,512]{1,0:T(8,128)} %get-tuple-element.77) | copy-start | bytes 1622020
  290.6 5.0 %collective-permute-start.10 = (bf16[33,256]{1,0:T(8,128)(2,1)S(1)}, bf16[33,256]{1,0:T(8,128)(2,1)S(1)}, u32[]{:S(2)}, u32[]{:S(2)}) collective-permute-start(bf16[33,256]{1,0:T(8,128)(2,1)S(1)} %get-tuple-element.202), channel_id=1, source_target_pairs={{0,6},{1,7},{2,0},{3,1},{4,2},{5,3},{6,4},{7,5},{8,14},{9,15},{10,... | collective-permute-start | bytes 50696 | tf_op jit(solution)/shard_map/ppermute | solution.py:438
  291.6 4.0 collective-permute-start.8
  292.1 4.1 collective-permute-start.9
  296.2 11.6 %collective-permute-start.11 = (bf16[97,256]{1,0:T(8,128)(2,1)S(1)}, bf16[97,256]{1,0:T(8,128)(2,1)S(1)}, u32[]{:S(2)}, u32[]{:S(2)}) collective-permute-start(bf16[97,256]{1,0:T(8,128)(2,1)S(1)} %pad_maximum_fusion.1), channel_id=1, source_target_pairs={{0,6},{1,7},{2,0},{3,1},{4,2},{5,3},{6,4},{7,5},{8,14},{9,15},{10,... | collective-permute-start | bytes 149000 | tf_op jit(solution)/shard_map/ppermute | solution.py:438
  298.1 41.1 %all-to-all-start.2 = ((bf16[8,33,512]{2,1,0:T(8,128)(2,1)}), bf16[8,33,512]{2,1,0:T(8,128)(2,1)}, u32[]{:S(2)}, u32[]{:S(2)}) async-start(bf16[8,33,512]{2,1,0:T(8,128)(2,1)} %convert_element_type.190), calls=%async_computation.2 | async-start | bytes 655360 | tf_op jit(solution)/shard_map/all_to_all | solution.py:424
  305.4 33.0 %copy-start.38 = (s32[256]{0:T(256)S(1)}, s32[256]{0:T(256)}, u32[]{:S(2)}) copy-start(s32[256]{0:T(256)} %owner_ref.1) | copy-start | bytes 3076
  305.4 63.4 %collective-permute-start.3 = (bf16[4,8,128,128]{3,2,1,0:T(8,128)(2,1)}, bf16[4,8,128,128]{3,2,1,0:T(8,128)(2,1)}, u32[]{:S(2)}, u32[]{:S(2)}) collective-permute-start(bf16[4,8,128,128]{3,2,1,0:T(8,128)(2,1)} %get-tuple-element.84), channel_id=1, source_target_pairs={{0,1},{1,0},{2,3},{3,2},{4,5},{5,4},{6,7},{7,6},{8,9},{9,8},{10,11... | collective-permute-start | bytes 3145736 | tf_op jit(solution)/shard_map/ppermute | solution.py:433
  305.7 8.8 %collective-permute-start.12 = (bf16[97,256]{1,0:T(8,128)(2,1)S(1)}, bf16[97,256]{1,0:T(8,128)(2,1)S(1)}, u32[]{:S(2)}, u32[]{:S(2)}) collective-permute-start(bf16[97,256]{1,0:T(8,128)(2,1)S(1)} %pad_maximum_fusion.1), channel_id=1, source_target_pairs={{0,4},{1,5},{2,6},{3,7},{4,0},{5,1},{6,2},{7,3},{8,12},{9,13},{10,... | collective-permute-start | bytes 149000 | tf_op jit(solution)/shard_map/ppermute | solution.py:438
  307.8 7.9 %collective-permute-start.13 = (bf16[97,256]{1,0:T(8,128)(2,1)S(1)}, bf16[97,256]{1,0:T(8,128)(2,1)S(1)}, u32[]{:S(2)}, u32[]{:S(2)}) collective-permute-start(bf16[97,256]{1,0:T(8,128)(2,1)S(1)} %pad_maximum_fusion.1), channel_id=1, source_target_pairs={{0,2},{1,3},{2,4},{3,5},{4,6},{5,7},{6,0},{7,1},{8,10},{9,11},{10,... | collective-permute-start | bytes 149000 | tf_op jit(solution)/shard_map/ppermute | solution.py:438
  316.5 19.3 %collective-permute-start.14 = (bf16[4,97,256]{2,1,0:T(8,128)(2,1)}, bf16[4,97,256]{2,1,0:T(8,128)(2,1)S(1)}, u32[]{:S(2)}, u32[]{:S(2)}) collective-permute-start(bf16[4,97,256]{2,1,0:T(8,128)(2,1)} %constant_dynamic-slice_fusion), channel_id=1, source_target_pairs={{0,1},{1,0},{2,3},{3,2},{4,5},{5,4},{6,7},{7,6},{8,9},{9,8},{10,11... | collective-permute-start | bytes 595976 | tf_op jit(solution)/shard_map/ppermute | solution.py:433
  316.5 31.1 %copy-start.10 = (bf16[2,64,1024]{2,1,0:T(8,128)(2,1)S(1)}, bf16[2,64,1024]{2,1,0:T(8,128)(2,1)}, u32[]{:S(2)}) copy-start(bf16[2,64,1024]{2,1,0:T(8,128)(2,1)} %copy-done.9) | copy-start | bytes 786436
  337.2 25.2 %collective-permute-start.15 = (bf16[8,97,256]{2,0,1:T(8,128)(2,1)}, bf16[8,97,256]{2,0,1:T(8,128)(2,1)}, u32[]{:S(2)}, u32[]{:S(2)}) collective-permute-start(bf16[8,97,256]{2,0,1:T(8,128)(2,1)} %select_n.174), channel_id=1, source_target_pairs={{0,16},{8,24},{16,0},{24,8},{1,17},{9,25},{17,1},{25,9},{2,18},{10... | collective-permute-start | bytes 1191944 | tf_op jit(solution)/shard_map/ppermute | solution.py:438
  341.0 12.5 %all-to-all-start.3 = ((f32[4,33,512]{2,1,0:T(8,128)}), f32[4,33,512]{2,1,0:T(8,128)}, u32[]{:S(2)}, u32[]{:S(2)}) async-start(f32[4,33,512]{2,1,0:T(8,128)} %broadcast_in_dim.78), calls=%async_computation.3 | async-start | bytes 655360 | tf_op jit(solution)/shard_map/all_to_all | solution.py:424
  356.7 19.1 %all-to-all-start.4 = ((bf16[8,33,512]{2,1,0:T(8,128)(2,1)}), bf16[8,33,512]{2,1,0:T(8,128)(2,1)}, u32[]{:S(2)}, u32[]{:S(2)}) async-start(bf16[8,33,512]{2,1,0:T(8,128)(2,1)} %broadcast_in_dim.79), calls=%async_computation.4 | async-start | bytes 655360 | tf_op jit(solution)/shard_map/all_to_all | solution.py:424
  367.3 44.8 %collective-permute-start.16 = (bf16[2,8,97,256]{3,1,2,0:T(8,128)(2,1)}, bf16[2,8,97,256]{3,1,2,0:T(8,128)(2,1)}, u32[]{:S(2)}, u32[]{:S(2)}) collective-permute-start(bf16[2,8,97,256]{3,1,2,0:T(8,128)(2,1)} %fusion.28), channel_id=1, source_target_pairs={{0,8},{8,0},{16,24},{24,16},{1,9},{9,1},{17,25},{25,17},{2,10},{10... | collective-permute-start | bytes 2383880 | tf_op jit(solution)/shard_map/ppermute | solution.py:433
  372.3 15.1 %collective-permute-start.4 = (bf16[8,128,128]{2,1,0:T(8,128)(2,1)}, bf16[8,128,128]{2,1,0:T(8,128)(2,1)}, u32[]{:S(2)}, u32[]{:S(2)}) collective-permute-start(bf16[8,128,128]{2,1,0:T(8,128)(2,1)} %get-tuple-element.194), channel_id=1, source_target_pairs={{0,2},{1,3},{2,4},{3,5},{4,6},{5,7},{6,0},{7,1},{8,10},{9,11},{10,... | collective-permute-start | bytes 786440 | tf_op jit(solution)/shard_map/ppermute | solution.py:438
  373.5 22.8 %collective-permute-start.5 = (bf16[8,128,128]{2,1,0:T(8,128)(2,1)}, bf16[8,128,128]{2,1,0:T(8,128)(2,1)}, u32[]{:S(2)}, u32[]{:S(2)}) collective-permute-start(bf16[8,128,128]{2,1,0:T(8,128)(2,1)} %get-tuple-element.196), channel_id=1, source_target_pairs={{0,4},{1,5},{2,6},{3,7},{4,0},{5,1},{6,2},{7,3},{8,12},{9,13},{10,... | collective-permute-start | bytes 786440 | tf_op jit(solution)/shard_map/ppermute | solution.py:438
  374.7 24.0 %collective-permute-start.6 = (bf16[8,128,128]{2,1,0:T(8,128)(2,1)}, bf16[8,128,128]{2,1,0:T(8,128)(2,1)}, u32[]{:S(2)}, u32[]{:S(2)}) collective-permute-start(bf16[8,128,128]{2,1,0:T(8,128)(2,1)} %get-tuple-element.195), channel_id=1, source_target_pairs={{0,6},{1,7},{2,0},{3,1},{4,2},{5,3},{6,4},{7,5},{8,14},{9,15},{10,... | collective-permute-start | bytes 786440 | tf_op jit(solution)/shard_map/ppermute | solution.py:438
  386.2 25.9 %copy-start.33 = (f32[2,1024]{1,0:T(2,128)}, f32[2,1024]{1,0:T(2,128)S(1)}, u32[]{:S(2)}) copy-start(f32[2,1024]{1,0:T(2,128)S(1)} %get-tuple-element.185) | copy-start | bytes 24580
  (33 other events, 159.6 us)
Sparse Core Ops, SparseCore 0:
  11.5 78.6 all-gather.1
